TPU v7x, 256 devices: a whole 4x4x8 slice. The times are simulated.
256 devices in a mesh: seq: 256 (over z, x, y, core).
Axes of the slice: x: 4, y: 4, z: 8, core: 2. Of those that a mesh axis runs over, the one named last changes fastest.
Arguments:
- queries: bfloat16 [131072, 4096], P('seq'), may hold values from -64 to 64
- keys: bfloat16 [131072, 512], P('seq'), may hold values from -64 to 64
- values: bfloat16 [131072, 512], P('seq'), may hold values from -6 to 6
- sink_logits: float32 [64], replicated, may hold values from 3 to 7
Outputs:
- attended: bfloat16 [131072, 4096], P('seq')
- sink_share: float32 [64], replicated
All inputs are finite; a program needn't handle non-finite values.
Results may differ from a plain program's by a relative error of at most 0.0042.
Values may be sent and summed in bfloat16 or wider, within the bound.
A program may use at most 128 MiB of HBM per device.

v0:
```python
import functools

import jax
import jax.numpy as jnp
from jax import lax
from jax.sharding import Mesh
from jax.sharding import PartitionSpec as P

HEAD_DIM = 64
WINDOW = 128
SINK_TOK = 512
SEQ = ("seq_0", "seq_1", "seq_2", "seq_3")


def from_behind(block, axis, distance):
    devices = range(lax.axis_size(axis))
    route = [(i - distance, i) for i in devices if i - distance in devices]
    return lax.ppermute(block, axis, route)


def one_axis_at_a_time(x, axes):
    return functools.reduce(lax.psum, axes, x)


def local(queries, keys, values, sink_logits):
    tok_rows = queries.shape[0]
    kv_width = keys.shape[1]
    kv_heads = kv_width // HEAD_DIM
    groups = queries.shape[1] // kv_width
    window = WINDOW
    sink_count = SINK_TOK
    blocks = tok_rows // window
    score_scale = HEAD_DIM ** (-0.5)
    devices = lax.axis_size(SEQ)
    dev_index = lax.axis_index(SEQ)
    row_start = dev_index * tok_rows
    edge_keys, edge_values = from_behind(
        (keys[tok_rows - window :], values[tok_rows - window :]), SEQ, 1
    )
    is_first = dev_index == 0
    hold_key = jnp.where(is_first, keys, jnp.zeros_like(keys))
    hold_value = jnp.where(is_first, values, jnp.zeros_like(values))
    for step_bit in range((devices - 1).bit_length()):
        got_key, got_value = from_behind((hold_key, hold_value), SEQ, 1 << step_bit)
        keep_own = dev_index < 1 << step_bit
        hold_key = jnp.where(keep_own, hold_key, got_key)
        hold_value = jnp.where(keep_own, hold_value, got_value)
    sink_key, sink_value = (hold_key, hold_value)
    extended_keys = jnp.concatenate([edge_keys, keys], axis=0).reshape(
        blocks + 1, window, kv_heads, HEAD_DIM
    )
    extended_values = jnp.concatenate([edge_values, values], axis=0).reshape(
        blocks + 1, window, kv_heads, HEAD_DIM
    )
    window_keys = jnp.concatenate([extended_keys[:-1], extended_keys[1:]], axis=1)
    window_values = jnp.concatenate([extended_values[:-1], extended_values[1:]], axis=1)
    window_keys = jnp.transpose(window_keys, (2, 0, 1, 3))
    window_values = jnp.transpose(window_values, (2, 0, 1, 3))
    sink_keys_heads = jnp.transpose(sink_key.reshape(sink_count, kv_heads, HEAD_DIM), (1, 0, 2))
    sink_values_heads = jnp.transpose(sink_value.reshape(sink_count, kv_heads, HEAD_DIM), (1, 0, 2))
    query_heads = jnp.transpose(
        queries.reshape(blocks, window, kv_heads, groups, HEAD_DIM), (2, 0, 1, 3, 4)
    )
    sink_heads = sink_logits.reshape(kv_heads, groups)
    block_start = row_start + window * jnp.arange(blocks, dtype=jnp.int32)
    query_pos = block_start[:, None] + jnp.arange(window, dtype=jnp.int32)[None, :]
    window_pos = block_start[:, None] - window + jnp.arange(2 * window, dtype=jnp.int32)[None, :]
    window_ok = (
        (window_pos[:, None, :] <= query_pos[:, :, None])
        & (window_pos[:, None, :] > query_pos[:, :, None] - window)
        & (window_pos[:, None, :] >= 0)
    )
    sink_pos = jnp.arange(sink_count, dtype=jnp.int32)
    sink_ok = sink_pos[None, None, :] <= query_pos[:, :, None] - window
    allowed = jnp.concatenate([sink_ok, window_ok], axis=2)

    def per_head(inputs):
        query_part, sink_kpart, sink_vpart, win_kpart, win_vpart, sink_part = inputs
        sink_scores = jnp.einsum(
            "btgd,sd->gbts", query_part, sink_kpart, preferred_element_type=jnp.float32
        )
        near_scores = jnp.einsum(
            "btgd,bsd->gbts", query_part, win_kpart, preferred_element_type=jnp.float32
        )
        scores = jnp.concatenate([sink_scores, near_scores], axis=3) * score_scale
        scores = jnp.where(allowed[None], scores, -jnp.inf)
        row_max = jnp.maximum(jnp.max(scores, axis=-1), sink_part[:, None, None])
        weight = jnp.exp(scores - row_max[..., None])
        sink_weight = jnp.exp(sink_part[:, None, None] - row_max)
        total = jnp.sum(weight, axis=-1) + sink_weight
        weight_bf = weight.astype(jnp.bfloat16)
        result = jnp.einsum(
            "gbts,sd->btgd",
            weight_bf[..., :sink_count],
            sink_vpart,
            preferred_element_type=jnp.float32,
        )
        result = result + jnp.einsum(
            "gbts,bsd->btgd",
            weight_bf[..., sink_count:],
            win_vpart,
            preferred_element_type=jnp.float32,
        )
        result = result / jnp.transpose(total, (1, 2, 0))[..., None]
        shares = jnp.sum(sink_weight / total, axis=(1, 2))
        return (result.astype(jnp.bfloat16), shares)

    outputs, head_shares = lax.map(
        per_head,
        (query_heads, sink_keys_heads, sink_values_heads, window_keys, window_values, sink_heads),
    )
    attended = jnp.transpose(outputs, (1, 2, 0, 3, 4)).reshape(
        tok_rows, kv_heads * groups * HEAD_DIM
    )
    summed = one_axis_at_a_time(head_shares, SEQ)
    sink_share = summed.reshape(kv_heads * groups) / (tok_rows * devices)
    return (attended, sink_share)


def solution(mesh):
    torus = Mesh(mesh.devices.reshape(8, 4, 4, 2), ("seq_0", "seq_1", "seq_2", "seq_3"))
    placed = (P(SEQ, None), P(SEQ, None), P(SEQ, None), P())
    return jax.shard_map(
        local, mesh=torus, in_specs=placed, out_specs=(P(SEQ, None), P()), check_vma=False
    )
```

profile of v0, /device:TPU:1, one launch (start us, length us, event | category | flops | bytes accessed | tf_op | source)
XLA Modules:
  0.0 528.9 jit_solution(4607979895430321398)
XLA Ops:
  1.5 4.6 collective-permute-start.16
  30.5 6.3 %collective-permute-done.9 = bf16[512,512]{1,0:T(8,128)(2,1)S(1)} collective-permute-done((bf16[512,512]{1,0:T(8,128)(2,1)S(1)}, bf16[512,512]{1,0:T(8,128)(2,1)S(1)}, u32[]{:S(2)}, u32[]{:S(2)}) %collective-permute-start.9) | collective-permute-done | bytes 524320 | tf_op jit(solution)/shard_map/ppermute | solution.py:18
  36.9 5.7 %collective-permute-start.10 = (bf16[512,512]{1,0:T(8,128)(2,1)S(1)}, bf16[512,512]{1,0:T(8,128)(2,1)S(1)}, u32[]{:S(2)}, u32[]{:S(2)}) collective-permute-start(bf16[512,512]{1,0:T(8,128)(2,1)S(1)} %broadcast_select_fusion.4), channel_id=1, source_target_pairs={{0,4},{1,5},{2,6},{3,7},{4,8},{5,9},{6,10},{7,11},{8,12},{9,13},{1... | collective-permute-start | bytes 1572872 | tf_op jit(solution)/shard_map/ppermute | solution.py:18
  42.6 5.5 %collective-permute-done.1 = bf16[512,512]{1,0:T(8,128)(2,1)} collective-permute-done((bf16[512,512]{1,0:T(8,128)(2,1)S(1)}, bf16[512,512]{1,0:T(8,128)(2,1)}, u32[]{:S(2)}, u32[]{:S(2)}) %collective-permute-start.1) | collective-permute-done | bytes 524320 | tf_op jit(solution)/shard_map/ppermute | solution.py:18
  48.2 7.4 %collective-permute-start.2 = (bf16[512,512]{1,0:T(8,128)(2,1)S(1)}, bf16[512,512]{1,0:T(8,128)(2,1)}, u32[]{:S(2)}, u32[]{:S(2)}) collective-permute-start(bf16[512,512]{1,0:T(8,128)(2,1)S(1)} %broadcast_select_fusion.5), channel_id=1, source_target_pairs={{0,4},{1,5},{2,6},{3,7},{4,8},{5,9},{6,10},{7,11},{8,12},{9,13},{1... | collective-permute-start | bytes 1572872 | tf_op jit(solution)/shard_map/ppermute | solution.py:18
  63.5 7.0 %collective-permute-done.2 = bf16[512,512]{1,0:T(8,128)(2,1)} collective-permute-done((bf16[512,512]{1,0:T(8,128)(2,1)S(1)}, bf16[512,512]{1,0:T(8,128)(2,1)}, u32[]{:S(2)}, u32[]{:S(2)}) %collective-permute-start.2) | collective-permute-done | bytes 524320 | tf_op jit(solution)/shard_map/ppermute | solution.py:18
  70.7 4.4 collective-permute-start.3
  75.1 4.5 collective-permute-start.12
  81.7 7.3 %collective-permute-start.4 = (bf16[512,512]{1,0:T(8,128)(2,1)}, bf16[512,512]{1,0:T(8,128)(2,1)}, u32[]{:S(2)}, u32[]{:S(2)}) collective-permute-start(bf16[512,512]{1,0:T(8,128)(2,1)} %broadcast_select_fusion.9), channel_id=1, source_target_pairs={{0,16},{1,17},{2,18},{3,19},{4,20},{5,21},{6,22},{7,23},{8,24},{9,... | collective-permute-start | bytes 1572872 | tf_op jit(solution)/shard_map/ppermute | solution.py:18
  89.2 15.0 %collective-permute-start.13 = (bf16[512,512]{1,0:T(8,128)(2,1)S(1)}, bf16[512,512]{1,0:T(8,128)(2,1)}, u32[]{:S(2)}, u32[]{:S(2)}) collective-permute-start(bf16[512,512]{1,0:T(8,128)(2,1)S(1)} %broadcast_select_fusion.10), channel_id=1, source_target_pairs={{0,32},{1,33},{2,34},{3,35},{4,36},{5,37},{6,38},{7,39},{8,40},{9,... | collective-permute-start | bytes 1572872 | tf_op jit(solution)/shard_map/ppermute | solution.py:18
  106.0 13.0 %collective-permute-start.5 = (bf16[512,512]{1,0:T(8,128)(2,1)}, bf16[512,512]{1,0:T(8,128)(2,1)}, u32[]{:S(2)}, u32[]{:S(2)}) collective-permute-start(bf16[512,512]{1,0:T(8,128)(2,1)} %broadcast_select_fusion.11), channel_id=1, source_target_pairs={{0,32},{1,33},{2,34},{3,35},{4,36},{5,37},{6,38},{7,39},{8,40},{9,... | collective-permute-start | bytes 1572872 | tf_op jit(solution)/shard_map/ppermute | solution.py:18
  119.2 5.9 %collective-permute-start.14 = (bf16[512,512]{1,0:T(8,128)(2,1)S(1)}, bf16[512,512]{1,0:T(8,128)(2,1)}, u32[]{:S(2)}, u32[]{:S(2)}) collective-permute-start(bf16[512,512]{1,0:T(8,128)(2,1)S(1)} %broadcast_select_fusion.12), channel_id=1, source_target_pairs={{0,64},{1,65},{2,66},{3,67},{4,68},{5,69},{6,70},{7,71},{8,72},{9,... | collective-permute-start | bytes 1572872 | tf_op jit(solution)/shard_map/ppermute | solution.py:18
  130.2 12.2 %collective-permute-start.6 = (bf16[512,512]{1,0:T(8,128)(2,1)S(1)}, bf16[512,512]{1,0:T(8,128)(2,1)}, u32[]{:S(2)}, u32[]{:S(2)}) collective-permute-start(bf16[512,512]{1,0:T(8,128)(2,1)S(1)} %broadcast_select_fusion.13), channel_id=1, source_target_pairs={{0,64},{1,65},{2,66},{3,67},{4,68},{5,69},{6,70},{7,71},{8,72},{9,... | collective-permute-start | bytes 1572872 | tf_op jit(solution)/shard_map/ppermute | solution.py:18
  147.0 6.4 %copy.19 = bf16[512,4096]{0,1:T(8,128)(2,1)} copy(bf16[512,4096]{1,0:T(8,128)(2,1)} %param.6) | data formatting | bytes 8388608 | tf_op args[0]
  153.4 6.9 %reshape.120 = bf16[4,128,8,8,64]{1,0,4,3,2:T(4,128)(2,1)} reshape(bf16[512,4096]{0,1:T(8,128)(2,1)} %copy.19) | data formatting | bytes 8388608 | tf_op jit(solution)/shard_map/reshape | solution.py:62
  161.5 12.6 %collective-permute-start.15 = (bf16[512,512]{1,0:T(8,128)(2,1)}, bf16[512,512]{1,0:T(8,128)(2,1)}, u32[]{:S(2)}, u32[]{:S(2)}) collective-permute-start(bf16[512,512]{1,0:T(8,128)(2,1)} %broadcast_select_fusion.14), channel_id=1, source_target_pairs={{0,128},{1,129},{2,130},{3,131},{4,132},{5,133},{6,134},{7,135},{8... | collective-permute-start | bytes 1572872 | tf_op jit(solution)/shard_map/ppermute | solution.py:18
  174.9 5.4 %collective-permute-start.7 = (bf16[512,512]{1,0:T(8,128)(2,1)}, bf16[512,512]{1,0:T(8,128)(2,1)}, u32[]{:S(2)}, u32[]{:S(2)}) collective-permute-start(bf16[512,512]{1,0:T(8,128)(2,1)} %broadcast_select_fusion.15), channel_id=1, source_target_pairs={{0,128},{1,129},{2,130},{3,131},{4,132},{5,133},{6,134},{7,135},{8... | collective-permute-start | bytes 1572872 | tf_op jit(solution)/shard_map/ppermute | solution.py:18
  188.9 203.0 %while.12 = (s32[]{:T(128)}, bf16[8,4,128,8,64]{2,4,1,3,0:T(8,128)(2,1)}, f32[8,8]{1,0:T(8,128)S(1)}, bf16[8,512,64]{1,2,0:T(8,128)(2,1)}, pred[4,128,768]{1,2,0...) while((s32[]{:T(128)}, ...), condition=%wide.region_4.5_spmd, body=%wide.region_0.4_spmd.sunk | while | flops 837566464 | bytes 56936292 | solution.py:108
  192.9 5.3 %convolution_bitcast_fusion.5 = f32[8,4,128,512]{2,3,0,1:T(8,128)} fusion(bf16[1,4,128,8,64]{2,1,4,3,0:T(4,128)(2,1)S(1)} %constant_dynamic-slice_fusion.6, bf16[8,512,64]{1,2,0:T(8,128)(2,1)} %get-tuple-element.207, s32[]{:T(128)} %get-tuple-element.190), kind=kOutput, calls=%fused_computation.8.clone.1 | convolution fusion | flops 268435456 | bytes 8978944 | tf_op jit(solution)/shard_map/while/body/eval_jaxpr/btgd,sd->gbts/dot_general | solution.py:79
  198.3 6.2 %fusion.55 = f32[8,4,128]{2,0,1:T(8,128)S(1)} fusion(f32[8,4,128,256]{2,3,0,1:T(8,128)} %convolution_bitcast_fusion.4, f32[8,4,128,512]{2,3,0,1:T(8,128)} %convolution_bitcast_fusion.5, pred[4,128,768]{1,2,0:T(8,128)(4,1)S(1)} %get-tuple-element.206), kind=kLoop, calls=%fused_computation.5.clone.1 | loop fusion | flops 12578816 | bytes 12992512 | tf_op jit(solution)/shard_map/while/body/eval_jaxpr/reduce_max | solution.py:87
  204.5 6.5 %fusion.57 = (f32[8,4,128]{2,0,1:T(8,128)S(1)}, bf16[8,4,128,768]{2,3,0,1:T(8,128)(2,1)S(1)}) fusion(f32[8,4,128]{2,0,1:T(8,128)S(1)} %broadcast_maximum_fusion.2, f32[8,4,128,256]{2,3,0,1:T(8,128)} %convolution_bitcast_fusion.4, f32[8,4,128,512]{2,3,0,1:T(8,128)} %convolution_bitcast_fusion.5, pred[4,128,768]{1,2,0:T(8,128)(4,1)S(1)} %get-tuple-element.206), kind=kLoop, calls=%fused_computation.3.clone.1 | loop fusion | flops 18870272 | bytes 19300352 | tf_op jit(solution)/shard_map/while/body/eval_jaxpr/reduce_sum | solution.py:90
  218.3 5.3 %convolution_bitcast_fusion.5 = f32[8,4,128,512]{2,3,0,1:T(8,128)} fusion(bf16[1,4,128,8,64]{2,1,4,3,0:T(4,128)(2,1)S(1)} %constant_dynamic-slice_fusion.6, bf16[8,512,64]{1,2,0:T(8,128)(2,1)} %get-tuple-element.207, s32[]{:T(128)} %get-tuple-element.190), kind=kOutput, calls=%fused_computation.8.clone.1 | convolution fusion | flops 268435456 | bytes 8978944 | tf_op jit(solution)/shard_map/while/body/eval_jaxpr/btgd,sd->gbts/dot_general | solution.py:79
  223.7 6.2 %fusion.55 = f32[8,4,128]{2,0,1:T(8,128)S(1)} fusion(f32[8,4,128,256]{2,3,0,1:T(8,128)} %convolution_bitcast_fusion.4, f32[8,4,128,512]{2,3,0,1:T(8,128)} %convolution_bitcast_fusion.5, pred[4,128,768]{1,2,0:T(8,128)(4,1)S(1)} %get-tuple-element.206), kind=kLoop, calls=%fused_computation.5.clone.1 | loop fusion | flops 12578816 | bytes 12992512 | tf_op jit(solution)/shard_map/while/body/eval_jaxpr/reduce_max | solution.py:87
  229.9 6.5 %fusion.57 = (f32[8,4,128]{2,0,1:T(8,128)S(1)}, bf16[8,4,128,768]{2,3,0,1:T(8,128)(2,1)S(1)}) fusion(f32[8,4,128]{2,0,1:T(8,128)S(1)} %broadcast_maximum_fusion.2, f32[8,4,128,256]{2,3,0,1:T(8,128)} %convolution_bitcast_fusion.4, f32[8,4,128,512]{2,3,0,1:T(8,128)} %convolution_bitcast_fusion.5, pred[4,128,768]{1,2,0:T(8,128)(4,1)S(1)} %get-tuple-element.206), kind=kLoop, calls=%fused_computation.3.clone.1 | loop fusion | flops 18870272 | bytes 19300352 | tf_op jit(solution)/shard_map/while/body/eval_jaxpr/reduce_sum | solution.py:90
  243.7 5.3 %convolution_bitcast_fusion.5 = f32[8,4,128,512]{2,3,0,1:T(8,128)} fusion(bf16[1,4,128,8,64]{2,1,4,3,0:T(4,128)(2,1)S(1)} %constant_dynamic-slice_fusion.6, bf16[8,512,64]{1,2,0:T(8,128)(2,1)} %get-tuple-element.207, s32[]{:T(128)} %get-tuple-element.190), kind=kOutput, calls=%fused_computation.8.clone.1 | convolution fusion | flops 268435456 | bytes 8978944 | tf_op jit(solution)/shard_map/while/body/eval_jaxpr/btgd,sd->gbts/dot_general | solution.py:79
  249.0 6.2 %fusion.55 = f32[8,4,128]{2,0,1:T(8,128)S(1)} fusion(f32[8,4,128,256]{2,3,0,1:T(8,128)} %convolution_bitcast_fusion.4, f32[8,4,128,512]{2,3,0,1:T(8,128)} %convolution_bitcast_fusion.5, pred[4,128,768]{1,2,0:T(8,128)(4,1)S(1)} %get-tuple-element.206), kind=kLoop, calls=%fused_computation.5.clone.1 | loop fusion | flops 12578816 | bytes 12992512 | tf_op jit(solution)/shard_map/while/body/eval_jaxpr/reduce_max | solution.py:87
  255.3 6.5 %fusion.57 = (f32[8,4,128]{2,0,1:T(8,128)S(1)}, bf16[8,4,128,768]{2,3,0,1:T(8,128)(2,1)S(1)}) fusion(f32[8,4,128]{2,0,1:T(8,128)S(1)} %broadcast_maximum_fusion.2, f32[8,4,128,256]{2,3,0,1:T(8,128)} %convolution_bitcast_fusion.4, f32[8,4,128,512]{2,3,0,1:T(8,128)} %convolution_bitcast_fusion.5, pred[4,128,768]{1,2,0:T(8,128)(4,1)S(1)} %get-tuple-element.206), kind=kLoop, calls=%fused_computation.3.clone.1 | loop fusion | flops 18870272 | bytes 19300352 | tf_op jit(solution)/shard_map/while/body/eval_jaxpr/reduce_sum | solution.py:90
  269.1 5.3 %convolution_bitcast_fusion.5 = f32[8,4,128,512]{2,3,0,1:T(8,128)} fusion(bf16[1,4,128,8,64]{2,1,4,3,0:T(4,128)(2,1)S(1)} %constant_dynamic-slice_fusion.6, bf16[8,512,64]{1,2,0:T(8,128)(2,1)} %get-tuple-element.207, s32[]{:T(128)} %get-tuple-element.190), kind=kOutput, calls=%fused_computation.8.clone.1 | convolution fusion | flops 268435456 | bytes 8978944 | tf_op jit(solution)/shard_map/while/body/eval_jaxpr/btgd,sd->gbts/dot_general | solution.py:79
  274.4 6.2 %fusion.55 = f32[8,4,128]{2,0,1:T(8,128)S(1)} fusion(f32[8,4,128,256]{2,3,0,1:T(8,128)} %convolution_bitcast_fusion.4, f32[8,4,128,512]{2,3,0,1:T(8,128)} %convolution_bitcast_fusion.5, pred[4,128,768]{1,2,0:T(8,128)(4,1)S(1)} %get-tuple-element.206), kind=kLoop, calls=%fused_computation.5.clone.1 | loop fusion | flops 12578816 | bytes 12992512 | tf_op jit(solution)/shard_map/while/body/eval_jaxpr/reduce_max | solution.py:87
  280.7 6.5 %fusion.57 = (f32[8,4,128]{2,0,1:T(8,128)S(1)}, bf16[8,4,128,768]{2,3,0,1:T(8,128)(2,1)S(1)}) fusion(f32[8,4,128]{2,0,1:T(8,128)S(1)} %broadcast_maximum_fusion.2, f32[8,4,128,256]{2,3,0,1:T(8,128)} %convolution_bitcast_fusion.4, f32[8,4,128,512]{2,3,0,1:T(8,128)} %convolution_bitcast_fusion.5, pred[4,128,768]{1,2,0:T(8,128)(4,1)S(1)} %get-tuple-element.206), kind=kLoop, calls=%fused_computation.3.clone.1 | loop fusion | flops 18870272 | bytes 19300352 | tf_op jit(solution)/shard_map/while/body/eval_jaxpr/reduce_sum | solution.py:90
  294.4 5.3 %convolution_bitcast_fusion.5 = f32[8,4,128,512]{2,3,0,1:T(8,128)} fusion(bf16[1,4,128,8,64]{2,1,4,3,0:T(4,128)(2,1)S(1)} %constant_dynamic-slice_fusion.6, bf16[8,512,64]{1,2,0:T(8,128)(2,1)} %get-tuple-element.207, s32[]{:T(128)} %get-tuple-element.190), kind=kOutput, calls=%fused_computation.8.clone.1 | convolution fusion | flops 268435456 | bytes 8978944 | tf_op jit(solution)/shard_map/while/body/eval_jaxpr/btgd,sd->gbts/dot_general | solution.py:79
  299.8 6.2 %fusion.55 = f32[8,4,128]{2,0,1:T(8,128)S(1)} fusion(f32[8,4,128,256]{2,3,0,1:T(8,128)} %convolution_bitcast_fusion.4, f32[8,4,128,512]{2,3,0,1:T(8,128)} %convolution_bitcast_fusion.5, pred[4,128,768]{1,2,0:T(8,128)(4,1)S(1)} %get-tuple-element.206), kind=kLoop, calls=%fused_computation.5.clone.1 | loop fusion | flops 12578816 | bytes 12992512 | tf_op jit(solution)/shard_map/while/body/eval_jaxpr/reduce_max | solution.py:87
  306.0 6.5 %fusion.57 = (f32[8,4,128]{2,0,1:T(8,128)S(1)}, bf16[8,4,128,768]{2,3,0,1:T(8,128)(2,1)S(1)}) fusion(f32[8,4,128]{2,0,1:T(8,128)S(1)} %broadcast_maximum_fusion.2, f32[8,4,128,256]{2,3,0,1:T(8,128)} %convolution_bitcast_fusion.4, f32[8,4,128,512]{2,3,0,1:T(8,128)} %convolution_bitcast_fusion.5, pred[4,128,768]{1,2,0:T(8,128)(4,1)S(1)} %get-tuple-element.206), kind=kLoop, calls=%fused_computation.3.clone.1 | loop fusion | flops 18870272 | bytes 19300352 | tf_op jit(solution)/shard_map/while/body/eval_jaxpr/reduce_sum | solution.py:90
  319.8 5.3 %convolution_bitcast_fusion.5 = f32[8,4,128,512]{2,3,0,1:T(8,128)} fusion(bf16[1,4,128,8,64]{2,1,4,3,0:T(4,128)(2,1)S(1)} %constant_dynamic-slice_fusion.6, bf16[8,512,64]{1,2,0:T(8,128)(2,1)} %get-tuple-element.207, s32[]{:T(128)} %get-tuple-element.190), kind=kOutput, calls=%fused_computation.8.clone.1 | convolution fusion | flops 268435456 | bytes 8978944 | tf_op jit(solution)/shard_map/while/body/eval_jaxpr/btgd,sd->gbts/dot_general | solution.py:79
  325.2 6.2 %fusion.55 = f32[8,4,128]{2,0,1:T(8,128)S(1)} fusion(f32[8,4,128,256]{2,3,0,1:T(8,128)} %convolution_bitcast_fusion.4, f32[8,4,128,512]{2,3,0,1:T(8,128)} %convolution_bitcast_fusion.5, pred[4,128,768]{1,2,0:T(8,128)(4,1)S(1)} %get-tuple-element.206), kind=kLoop, calls=%fused_computation.5.clone.1 | loop fusion | flops 12578816 | bytes 12992512 | tf_op jit(solution)/shard_map/while/body/eval_jaxpr/reduce_max | solution.py:87
  331.4 6.5 %fusion.57 = (f32[8,4,128]{2,0,1:T(8,128)S(1)}, bf16[8,4,128,768]{2,3,0,1:T(8,128)(2,1)S(1)}) fusion(f32[8,4,128]{2,0,1:T(8,128)S(1)} %broadcast_maximum_fusion.2, f32[8,4,128,256]{2,3,0,1:T(8,128)} %convolution_bitcast_fusion.4, f32[8,4,128,512]{2,3,0,1:T(8,128)} %convolution_bitcast_fusion.5, pred[4,128,768]{1,2,0:T(8,128)(4,1)S(1)} %get-tuple-element.206), kind=kLoop, calls=%fused_computation.3.clone.1 | loop fusion | flops 18870272 | bytes 19300352 | tf_op jit(solution)/shard_map/while/body/eval_jaxpr/reduce_sum | solution.py:90
  345.2 5.3 %convolution_bitcast_fusion.5 = f32[8,4,128,512]{2,3,0,1:T(8,128)} fusion(bf16[1,4,128,8,64]{2,1,4,3,0:T(4,128)(2,1)S(1)} %constant_dynamic-slice_fusion.6, bf16[8,512,64]{1,2,0:T(8,128)(2,1)} %get-tuple-element.207, s32[]{:T(128)} %get-tuple-element.190), kind=kOutput, calls=%fused_computation.8.clone.1 | convolution fusion | flops 268435456 | bytes 8978944 | tf_op jit(solution)/shard_map/while/body/eval_jaxpr/btgd,sd->gbts/dot_general | solution.py:79
  350.5 6.2 %fusion.55 = f32[8,4,128]{2,0,1:T(8,128)S(1)} fusion(f32[8,4,128,256]{2,3,0,1:T(8,128)} %convolution_bitcast_fusion.4, f32[8,4,128,512]{2,3,0,1:T(8,128)} %convolution_bitcast_fusion.5, pred[4,128,768]{1,2,0:T(8,128)(4,1)S(1)} %get-tuple-element.206), kind=kLoop, calls=%fused_computation.5.clone.1 | loop fusion | flops 12578816 | bytes 12992512 | tf_op jit(solution)/shard_map/while/body/eval_jaxpr/reduce_max | solution.py:87
  356.8 6.5 %fusion.57 = (f32[8,4,128]{2,0,1:T(8,128)S(1)}, bf16[8,4,128,768]{2,3,0,1:T(8,128)(2,1)S(1)}) fusion(f32[8,4,128]{2,0,1:T(8,128)S(1)} %broadcast_maximum_fusion.2, f32[8,4,128,256]{2,3,0,1:T(8,128)} %convolution_bitcast_fusion.4, f32[8,4,128,512]{2,3,0,1:T(8,128)} %convolution_bitcast_fusion.5, pred[4,128,768]{1,2,0:T(8,128)(4,1)S(1)} %get-tuple-element.206), kind=kLoop, calls=%fused_computation.3.clone.1 | loop fusion | flops 18870272 | bytes 19300352 | tf_op jit(solution)/shard_map/while/body/eval_jaxpr/reduce_sum | solution.py:90
  370.6 5.3 %convolution_bitcast_fusion.5 = f32[8,4,128,512]{2,3,0,1:T(8,128)} fusion(bf16[1,4,128,8,64]{2,1,4,3,0:T(4,128)(2,1)S(1)} %constant_dynamic-slice_fusion.6, bf16[8,512,64]{1,2,0:T(8,128)(2,1)} %get-tuple-element.207, s32[]{:T(128)} %get-tuple-element.190), kind=kOutput, calls=%fused_computation.8.clone.1 | convolution fusion | flops 268435456 | bytes 8978944 | tf_op jit(solution)/shard_map/while/body/eval_jaxpr/btgd,sd->gbts/dot_general | solution.py:79
  375.9 6.2 %fusion.55 = f32[8,4,128]{2,0,1:T(8,128)S(1)} fusion(f32[8,4,128,256]{2,3,0,1:T(8,128)} %convolution_bitcast_fusion.4, f32[8,4,128,512]{2,3,0,1:T(8,128)} %convolution_bitcast_fusion.5, pred[4,128,768]{1,2,0:T(8,128)(4,1)S(1)} %get-tuple-element.206), kind=kLoop, calls=%fused_computation.5.clone.1 | loop fusion | flops 12578816 | bytes 12992512 | tf_op jit(solution)/shard_map/while/body/eval_jaxpr/reduce_max | solution.py:87
  382.2 6.5 %fusion.57 = (f32[8,4,128]{2,0,1:T(8,128)S(1)}, bf16[8,4,128,768]{2,3,0,1:T(8,128)(2,1)S(1)}) fusion(f32[8,4,128]{2,0,1:T(8,128)S(1)} %broadcast_maximum_fusion.2, f32[8,4,128,256]{2,3,0,1:T(8,128)} %convolution_bitcast_fusion.4, f32[8,4,128,512]{2,3,0,1:T(8,128)} %convolution_bitcast_fusion.5, pred[4,128,768]{1,2,0:T(8,128)(4,1)S(1)} %get-tuple-element.206), kind=kLoop, calls=%fused_computation.3.clone.1 | loop fusion | flops 18870272 | bytes 19300352 | tf_op jit(solution)/shard_map/while/body/eval_jaxpr/reduce_sum | solution.py:90
  391.9 13.0 %copy.37 = bf16[4,128,8,8,64]{4,3,2,1,0:T(8,128)(2,1)} copy(bf16[4,128,8,8,64]{1,4,0,3,2:T(8,128)(2,1)} %bitcast.106) | data formatting | bytes 8388608
  404.9 12.0 %reshape.127 = bf16[512,4096]{1,0:T(8,128)(2,1)} reshape(bf16[4,128,8,8,64]{4,3,2,1,0:T(8,128)(2,1)} %copy.37) | data formatting | bytes 8388608
  417.0 47.0 %psum.28 = f32[8,8]{1,0:T(8,128)S(1)} all-reduce(f32[8,8]{1,0:T(8,128)S(1)} %get-tuple-element.56), channel_id=1, replica_groups=mesh['seq_0'=8,'seq_1'=4,'seq_2'=4,'seq_3'=2] {'seq_0'}, use_global_device_ids=true, to_apply=%region_5.6 | all-reduce | flops 64 | bytes 512 | tf_op jit(solution)/shard_map/psum | solution.py:22
  464.0 17.5 %psum.29 = f32[8,8]{1,0:T(8,128)S(1)} all-reduce(f32[8,8]{1,0:T(8,128)S(1)} %psum.28), channel_id=1, replica_groups=mesh['seq_0'=8,'seq_1'=4,'seq_2'=4,'seq_3'=2] {'seq_1'}, use_global_device_ids=true, to_apply=%region_6.7 | all-reduce | flops 64 | bytes 512 | tf_op jit(solution)/shard_map/psum | solution.py:22
  481.5 9.2 %psum.30 = f32[8,8]{1,0:T(8,128)S(1)} all-reduce(f32[8,8]{1,0:T(8,128)S(1)} %psum.29), channel_id=1, replica_groups=mesh['seq_0'=8,'seq_1'=4,'seq_2'=4,'seq_3'=2] {'seq_2'}, use_global_device_ids=true, to_apply=%region_7.8 | all-reduce | flops 64 | bytes 512 | tf_op jit(solution)/shard_map/psum | solution.py:22
  490.7 37.6 %psum.31 = f32[8,8]{1,0:T(8,128)S(1)} all-reduce(f32[8,8]{1,0:T(8,128)S(1)} %psum.30), channel_id=1, replica_groups=mesh['seq_0'=8,'seq_1'=4,'seq_2'=4,'seq_3'=2] {'seq_3'}, use_global_device_ids=true, to_apply=%region_8.9 | all-reduce | flops 64 | bytes 512 | tf_op jit(solution)/shard_map/psum | solution.py:22
  (150 shorter events, 116.7 us)
Async XLA Ops:
  1.5 7.5 %collective-permute-start.16 = (bf16[128,512]{1,0:T(8,128)(2,1)S(1)}, bf16[128,512]{1,0:T(8,128)(2,1)S(1)}, u32[]{:S(2)}, u32[]{:S(2)}) collective-permute-start(bf16[128,512]{1,0:T(8,128)(2,1)S(1)} %slice.32), channel_id=1, source_target_pairs={{0,1},{1,2},{2,3},{3,4},{4,5},{5,6},{6,7},{7,8},{8,9},{9,10},{10,1... | collective-permute-start | bytes 393224 | tf_op jit(solution)/shard_map/ppermute | solution.py:18
  7.1 6.8 %collective-permute-start.17 = (bf16[128,512]{1,0:T(8,128)(2,1)S(1)}, bf16[128,512]{1,0:T(8,128)(2,1)S(1)}, u32[]{:S(2)}, u32[]{:S(2)}) collective-permute-start(bf16[128,512]{1,0:T(8,128)(2,1)S(1)} %slice.36), channel_id=1, source_target_pairs={{0,1},{1,2},{2,3},{3,4},{4,5},{5,6},{6,7},{7,8},{8,9},{9,10},{10,1... | collective-permute-start | bytes 393224 | tf_op jit(solution)/shard_map/ppermute | solution.py:18
  10.3 9.7 %collective-permute-start.8 = (bf16[512,512]{1,0:T(8,128)(2,1)S(1)}, bf16[512,512]{1,0:T(8,128)(2,1)S(1)}, u32[]{:S(2)}, u32[]{:S(2)}) collective-permute-start(bf16[512,512]{1,0:T(8,128)(2,1)S(1)} %get-tuple-element.98), channel_id=1, source_target_pairs={{0,1},{1,2},{2,3},{3,4},{4,5},{5,6},{6,7},{7,8},{8,9},{9,10},{10,1... | collective-permute-start | bytes 1572872 | tf_op jit(solution)/shard_map/ppermute | solution.py:18
  15.2 10.4 %collective-permute-start = (bf16[512,512]{1,0:T(8,128)(2,1)S(1)}, bf16[512,512]{1,0:T(8,128)(2,1)}, u32[]{:S(2)}, u32[]{:S(2)}) collective-permute-start(bf16[512,512]{1,0:T(8,128)(2,1)S(1)} %get-tuple-element.96), channel_id=1, source_target_pairs={{0,1},{1,2},{2,3},{3,4},{4,5},{5,6},{6,7},{7,8},{8,9},{9,10},{10,1... | collective-permute-start | bytes 1572872 | tf_op jit(solution)/shard_map/ppermute | solution.py:18
  20.1 16.8 %collective-permute-start.9 = (bf16[512,512]{1,0:T(8,128)(2,1)S(1)}, bf16[512,512]{1,0:T(8,128)(2,1)S(1)}, u32[]{:S(2)}, u32[]{:S(2)}) collective-permute-start(bf16[512,512]{1,0:T(8,128)(2,1)S(1)} %broadcast_select_fusion.2), channel_id=1, source_target_pairs={{0,2},{1,3},{2,4},{3,5},{4,6},{5,7},{6,8},{7,9},{8,10},{9,11},{10,... | collective-permute-start | bytes 1572872 | tf_op jit(solution)/shard_map/ppermute | solution.py:18
  26.7 21.4 %collective-permute-start.1 = (bf16[512,512]{1,0:T(8,128)(2,1)S(1)}, bf16[512,512]{1,0:T(8,128)(2,1)}, u32[]{:S(2)}, u32[]{:S(2)}) collective-permute-start(bf16[512,512]{1,0:T(8,128)(2,1)S(1)} %broadcast_select_fusion.3), channel_id=1, source_target_pairs={{0,2},{1,3},{2,4},{3,5},{4,6},{5,7},{6,8},{7,9},{8,10},{9,11},{10,... | collective-permute-start | bytes 1572872 | tf_op jit(solution)/shard_map/ppermute | solution.py:18
  36.9 22.4 %collective-permute-start.10 = (bf16[512,512]{1,0:T(8,128)(2,1)S(1)}, bf16[512,512]{1,0:T(8,128)(2,1)S(1)}, u32[]{:S(2)}, u32[]{:S(2)}) collective-permute-start(bf16[512,512]{1,0:T(8,128)(2,1)S(1)} %broadcast_select_fusion.4), channel_id=1, source_target_pairs={{0,4},{1,5},{2,6},{3,7},{4,8},{5,9},{6,10},{7,11},{8,12},{9,13},{1... | collective-permute-start | bytes 1572872 | tf_op jit(solution)/shard_map/ppermute | solution.py:18
  48.2 22.4 %collective-permute-start.2 = (bf16[512,512]{1,0:T(8,128)(2,1)S(1)}, bf16[512,512]{1,0:T(8,128)(2,1)}, u32[]{:S(2)}, u32[]{:S(2)}) collective-permute-start(bf16[512,512]{1,0:T(8,128)(2,1)S(1)} %broadcast_select_fusion.5), channel_id=1, source_target_pairs={{0,4},{1,5},{2,6},{3,7},{4,8},{5,9},{6,10},{7,11},{8,12},{9,13},{1... | collective-permute-start | bytes 1572872 | tf_op jit(solution)/shard_map/ppermute | solution.py:18
  59.4 15.6 %collective-permute-start.11 = (bf16[512,512]{1,0:T(8,128)(2,1)S(1)}, bf16[512,512]{1,0:T(8,128)(2,1)S(1)}, u32[]{:S(2)}, u32[]{:S(2)}) collective-permute-start(bf16[512,512]{1,0:T(8,128)(2,1)S(1)} %broadcast_select_fusion.6), channel_id=1, source_target_pairs={{0,8},{1,9},{2,10},{3,11},{4,12},{5,13},{6,14},{7,15},{8,16},{9,17... | collective-permute-start | bytes 1572872 | tf_op jit(solution)/shard_map/ppermute | solution.py:18
  70.7 10.2 %collective-permute-start.3 = (bf16[512,512]{1,0:T(8,128)(2,1)S(1)}, bf16[512,512]{1,0:T(8,128)(2,1)}, u32[]{:S(2)}, u32[]{:S(2)}) collective-permute-start(bf16[512,512]{1,0:T(8,128)(2,1)S(1)} %broadcast_select_fusion.7), channel_id=1, source_target_pairs={{0,8},{1,9},{2,10},{3,11},{4,12},{5,13},{6,14},{7,15},{8,16},{9,17... | collective-permute-start | bytes 1572872 | tf_op jit(solution)/shard_map/ppermute | solution.py:18
  75.1 67.7 %copy-start = (bf16[512,512]{1,0:T(8,128)(2,1)S(1)}, bf16[512,512]{1,0:T(8,128)(2,1)}, u32[]{:S(2)}) copy-start(bf16[512,512]{1,0:T(8,128)(2,1)} %param.7) | copy-start | bytes 1572868
  75.1 68.7 %copy-start.1 = (bf16[512,512]{1,0:T(8,128)(2,1)S(1)}, bf16[512,512]{1,0:T(8,128)(2,1)}, u32[]{:S(2)}) copy-start(bf16[512,512]{1,0:T(8,128)(2,1)} %param.8) | copy-start | bytes 1572868
  75.1 14.0 %collective-permute-start.12 = (bf16[512,512]{1,0:T(8,128)(2,1)S(1)}, bf16[512,512]{1,0:T(8,128)(2,1)}, u32[]{:S(2)}, u32[]{:S(2)}) collective-permute-start(bf16[512,512]{1,0:T(8,128)(2,1)S(1)} %broadcast_select_fusion.8), channel_id=1, source_target_pairs={{0,16},{1,17},{2,18},{3,19},{4,20},{5,21},{6,22},{7,23},{8,24},{9,... | collective-permute-start | bytes 1572872 | tf_op jit(solution)/shard_map/ppermute | solution.py:18
  81.7 22.4 %collective-permute-start.4 = (bf16[512,512]{1,0:T(8,128)(2,1)}, bf16[512,512]{1,0:T(8,128)(2,1)}, u32[]{:S(2)}, u32[]{:S(2)}) collective-permute-start(bf16[512,512]{1,0:T(8,128)(2,1)} %broadcast_select_fusion.9), channel_id=1, source_target_pairs={{0,16},{1,17},{2,18},{3,19},{4,20},{5,21},{6,22},{7,23},{8,24},{9,... | collective-permute-start | bytes 1572872 | tf_op jit(solution)/shard_map/ppermute | solution.py:18
  89.2 30.0 %collective-permute-start.13 = (bf16[512,512]{1,0:T(8,128)(2,1)S(1)}, bf16[512,512]{1,0:T(8,128)(2,1)}, u32[]{:S(2)}, u32[]{:S(2)}) collective-permute-start(bf16[512,512]{1,0:T(8,128)(2,1)S(1)} %broadcast_select_fusion.10), channel_id=1, source_target_pairs={{0,32},{1,33},{2,34},{3,35},{4,36},{5,37},{6,38},{7,39},{8,40},{9,... | collective-permute-start | bytes 1572872 | tf_op jit(solution)/shard_map/ppermute | solution.py:18
  106.0 23.1 %collective-permute-start.5 = (bf16[512,512]{1,0:T(8,128)(2,1)}, bf16[512,512]{1,0:T(8,128)(2,1)}, u32[]{:S(2)}, u32[]{:S(2)}) collective-permute-start(bf16[512,512]{1,0:T(8,128)(2,1)} %broadcast_select_fusion.11), channel_id=1, source_target_pairs={{0,32},{1,33},{2,34},{3,35},{4,36},{5,37},{6,38},{7,39},{8,40},{9,... | collective-permute-start | bytes 1572872 | tf_op jit(solution)/shard_map/ppermute | solution.py:18
  119.2 41.4 %collective-permute-start.14 = (bf16[512,512]{1,0:T(8,128)(2,1)S(1)}, bf16[512,512]{1,0:T(8,128)(2,1)}, u32[]{:S(2)}, u32[]{:S(2)}) collective-permute-start(bf16[512,512]{1,0:T(8,128)(2,1)S(1)} %broadcast_select_fusion.12), channel_id=1, source_target_pairs={{0,64},{1,65},{2,66},{3,67},{4,68},{5,69},{6,70},{7,71},{8,72},{9,... | collective-permute-start | bytes 1572872 | tf_op jit(solution)/shard_map/ppermute | solution.py:18
  130.2 43.9 %collective-permute-start.6 = (bf16[512,512]{1,0:T(8,128)(2,1)S(1)}, bf16[512,512]{1,0:T(8,128)(2,1)}, u32[]{:S(2)}, u32[]{:S(2)}) collective-permute-start(bf16[512,512]{1,0:T(8,128)(2,1)S(1)} %broadcast_select_fusion.13), channel_id=1, source_target_pairs={{0,64},{1,65},{2,66},{3,67},{4,68},{5,69},{6,70},{7,71},{8,72},{9,... | collective-permute-start | bytes 1572872 | tf_op jit(solution)/shard_map/ppermute | solution.py:18
  153.4 6.9 %copy-start.2 = (f32[64]{0:T(128)S(1)}, f32[64]{0:T(128)}, u32[]{:S(2)}) copy-start(f32[64]{0:T(128)} %param.9) | copy-start | bytes 772
  161.5 23.2 %collective-permute-start.15 = (bf16[512,512]{1,0:T(8,128)(2,1)}, bf16[512,512]{1,0:T(8,128)(2,1)}, u32[]{:S(2)}, u32[]{:S(2)}) collective-permute-start(bf16[512,512]{1,0:T(8,128)(2,1)} %broadcast_select_fusion.14), channel_id=1, source_target_pairs={{0,128},{1,129},{2,130},{3,131},{4,132},{5,133},{6,134},{7,135},{8... | collective-permute-start | bytes 1572872 | tf_op jit(solution)/shard_map/ppermute | solution.py:18
  174.9 11.9 %collective-permute-start.7 = (bf16[512,512]{1,0:T(8,128)(2,1)}, bf16[512,512]{1,0:T(8,128)(2,1)}, u32[]{:S(2)}, u32[]{:S(2)}) collective-permute-start(bf16[512,512]{1,0:T(8,128)(2,1)} %broadcast_select_fusion.15), channel_id=1, source_target_pairs={{0,128},{1,129},{2,130},{3,131},{4,132},{5,133},{6,134},{7,135},{8... | collective-permute-start | bytes 1572872 | tf_op jit(solution)/shard_map/ppermute | solution.py:18
where the time goes:
time: 532 us; the launch traced here: 529 us
  other arithmetic  119 us (22%)
  starting transfers between devices  116 us (22%)
  blocking collectives  111 us (21%)
  matrix products  87.8 us (17%)
  local copies, waits for them, and re-layouts  59.5 us (11%)
  waiting for transfers between devices  33.3 us (6%)
    ppermute x18, starting transfers between devices, from_behind(): return lax.ppermute(block, axis, route)  116 us
    psum x4, blocking collectives, one_axis_at_a_time(): return functools.reduce(lax.psum, axes, x)  111 us
    reduce_sum x8, other arithmetic, per_head(): total = jnp.sum(weight, axis=-1) + sink_weight  52.4 us
    reduce_max x8, other arithmetic, per_head(): row_max = jnp.maximum(jnp.max(scores, axis=-1), sink_part[:, None, None])  49.3 us
    dot_general x8, matrix products, per_head(): jnp.einsum('btgd,sd->gbts', query_part, sink_kpart, preferred_element_typ...  42.7 us
    ppermute x18, waiting for transfers between devices, from_behind(): return lax.ppermute(block, axis, route)  33.3 us
    unnamed x11, local copies, waits for them, and re-layouts  32.8 us
    dot_general x8, matrix products, per_head(): jnp.einsum('btgd,bsd->gbts', query_part, win_kpart, preferred_element_typ...  21.4 us
  transfers between devices with their start and end apart: 18, of which 8 were waited for; matrix products, arithmetic and copies ran while one was open for 7% of the time, Pallas kernels for 0%

commit v1 on v0

v1 whole, which is shorter than its diff:
```python
import functools

import jax
import jax.numpy as jnp
from jax import lax
from jax.experimental import pallas as pl
from jax.experimental.pallas import tpu as pltpu
from jax.sharding import Mesh
from jax.sharding import PartitionSpec as P

HEAD_DIM = 64
WINDOW = 128
SINK_TOK = 512
AXES = ("seq_0", "seq_1", "seq_2", "seq_3")
SIZES = (8, 4, 4, 2)
MESH = pl.DeviceIdType.MESH
F32 = jnp.float32
BF16 = jnp.bfloat16
NEG = -1e30
EXP_SCALE = 1.4426950408889634 / 8.0
PIECE = 32


def where_am_i():
    z, x, y, c = (lax.axis_index(a) for a in AXES)
    return z, x, y, c, ((z * 4 + x) * 4 + y) * 2 + c


def coords(lin):
    return (lin // 32, lax.rem(lin // 8, 4), lax.rem(lin // 2, 4), lax.rem(lin, 2))


def plane_peer(z, x, y, c, step):
    return (z, lax.rem(x + step // 4, 4), lax.rem(y + step % 4, 4), c)


def signal(sem, device):
    pl.semaphore_signal(sem, inc=1, device_id=device, device_id_type=MESH)


def spread_kernel(k_ref, v_ref, kv, edge, s1, r1, s2, r2, s3, r3, s4, r4, se, re, sl):
    z, x, y, c, lin = where_am_i()
    xy = 4 * x + y
    first = lin == 0
    relay = z == 0
    rows = pl.ds(pl.multiple_of(xy * PIECE, PIECE), PIECE)

    def remote(src, dst, send, recv, device):
        return pltpu.make_async_remote_copy(
            src_ref=src, dst_ref=dst, send_sem=send, recv_sem=recv, device_id=device, device_id_type=MESH
        )

    barrier = pltpu.get_barrier_semaphore()
    for step in range(1, 16):
        signal(barrier, plane_peer(z, x, y, c, step))
    signal(barrier, (z, x, y, 1 - c))

    @pl.when(lin > 0)
    def _():
        signal(barrier, coords(lin - 1))

    @pl.when(z > 0)
    def _():
        signal(barrier, (0, x, y, c))

    @pl.when(relay & (lin > 0))
    def _():
        signal(barrier, (0, 0, 0, 0))

    waits = 16 + jnp.where(lin < 255, 1, 0) + jnp.where(relay, 7, 0) + jnp.where(first, 31, 0)
    pl.semaphore_wait(barrier, waits)

    @pl.when(first)
    def _():
        for cc, ref in ((0, k_ref), (1, v_ref)):
            for p in range(16):
                part = pl.ds(p * PIECE, PIECE)
                if cc == 0 and p == 0:
                    pltpu.make_async_copy(ref.at[part], kv.at[cc, part], r1).start()
                else:
                    remote(ref.at[part], kv.at[cc, part], s1, r1, (0, p // 4, p % 4, cc)).start()

    @pl.when(lin < 255)
    def _():
        for cc, ref in ((0, k_ref), (1, v_ref)):
            remote(ref.at[pl.ds(384, 128)], edge.at[cc], se.at[cc], re.at[cc], coords(lin + 1)).start()

    @pl.when(first)
    def _():
        for cc, ref in ((0, k_ref), (1, v_ref)):
            pltpu.make_async_copy(ref.at[pl.ds(0, 128)], edge.at[cc], sl.at[cc]).start()

    @pl.when(relay)
    def _():
        remote(kv.at[c, rows], kv.at[c, rows], s2, r1, (z, x, y, c)).wait_recv()
        for zz in range(1, 8):
            remote(kv.at[c, rows], kv.at[c, rows], s2, r2, (zz, x, y, c)).start()

    @pl.when(z > 0)
    def _():
        remote(kv.at[c, rows], kv.at[c, rows], s2, r2, (z, x, y, c)).wait_recv()

    for step in range(1, 16):
        remote(kv.at[c, rows], kv.at[c, rows], s3, r3, plane_peer(z, x, y, c, step)).start()
    all15 = kv.at[c, pl.ds(0, 15 * PIECE)]
    remote(all15, all15, s3, r3, (z, x, y, c)).wait_recv()
    half = remote(kv.at[c], kv.at[c], s4, r4, (z, x, y, 1 - c))
    half.start()
    half.wait_recv()
    half.wait_send()
    remote(all15, all15, s3, r3, (z, x, y, c)).wait_send()

    @pl.when(relay)
    def _():
        seven = kv.at[c, pl.ds(0, 7 * PIECE)]
        remote(seven, seven, s2, r2, (z, x, y, c)).wait_send()

    @pl.when(first)
    def _():
        many = kv.at[:, pl.ds(0, 496)]
        remote(many, many, s1, r1, (z, x, y, c)).wait_send()
        for cc, ref in ((0, k_ref), (1, v_ref)):
            pltpu.make_async_copy(ref.at[pl.ds(0, 128)], edge.at[cc], sl.at[cc]).wait()

    @pl.when(lin < 255)
    def _():
        for cc, ref in ((0, k_ref), (1, v_ref)):
            remote(ref.at[pl.ds(384, 128)], edge.at[cc], se.at[cc], re.at[cc], coords(lin + 1)).wait_send()

    @pl.when(lin > 0)
    def _():
        for cc, ref in ((0, k_ref), (1, v_ref)):
            remote(ref.at[pl.ds(384, 128)], edge.at[cc], se.at[cc], re.at[cc], coords(lin)).wait_recv()


def spread(keys, values):
    vmem = pl.BlockSpec(memory_space=pltpu.VMEM)
    dma = pltpu.SemaphoreType.DMA
    return pl.pallas_call(
        spread_kernel,
        in_specs=[pl.BlockSpec(memory_space=pl.ANY)] * 2,
        out_specs=[vmem, vmem],
        out_shape=[
            jax.ShapeDtypeStruct((2, SINK_TOK, 512), BF16),
            jax.ShapeDtypeStruct((2, WINDOW, 512), BF16),
        ],
        scratch_shapes=[dma(())] * 8 + [dma((2,))] * 3,
        compiler_params=pltpu.CompilerParams(collective_id=0, has_side_effects=True),
    )(keys, values)


def pad_heads(tile):
    low = lax.broadcasted_iota(jnp.int32, tile.shape, 1) < 64
    wide = tile.astype(F32)
    first = jnp.where(low, wide, 0.0)
    second = jnp.where(low, 0.0, wide)
    turned_first = pltpu.roll(first, 64, 1)
    turned_second = pltpu.roll(second, 64, 1)
    return ((first.astype(BF16), turned_first.astype(BF16)), (turned_second.astype(BF16), second.astype(BF16)))


def attend_kernel(sink_ref, q_hbm, kv_ref, edge_ref, k_ref, v_ref, o_hbm, sh_ref, qb, ob, kp, vp, sq, so):
    _, _, _, _, lin = where_am_i()
    for g in range(8):
        cols = pl.ds(g * 512, 512)
        pltpu.make_async_copy(q_hbm.at[:, cols], qb.at[g], sq.at[g]).start()

    low = lax.broadcasted_iota(jnp.int32, (1, 128), 1) < 64
    row = lax.broadcasted_iota(jnp.int32, (128, 128), 0)
    col = lax.broadcasted_iota(jnp.int32, (128, 128), 1)
    own = col <= row
    ones = (jnp.where(low, 1.0, 0.0).astype(BF16), jnp.where(low, 0.0, 1.0).astype(BF16))
    contract_last = (((1,), (1,)), ((), ()))

    def group(g, special):
        pair_cols = pl.ds(pl.multiple_of((g // 2) * 128, 128), 128)

        def prepare(half):
            for which, dst, ref in ((0, kp, k_ref), (1, vp, v_ref)):
                for start, src in (
                    (0, kv_ref.at[which]),
                    (SINK_TOK, edge_ref.at[which]),
                    (SINK_TOK + WINDOW, ref),
                ):
                    made = pad_heads(src[:, pair_cols])[half]
                    size = made[0].shape[0]
                    dst[0, start : start + size, :] = made[0]
                    dst[1, start : start + size, :] = made[1]

        @pl.when(lax.rem(g, 2) == 0)
        def _():
            prepare(0)

        @pl.when(lax.rem(g, 2) == 1)
        def _():
            prepare(1)

        pltpu.make_async_copy(q_hbm.at[:, pl.ds(0, 512)], qb.at[g], sq.at[g]).wait()

        share = [jnp.zeros((1, 128), F32) for _ in range(4)]
        for b in range(4):
            for p in range(4):
                q = qb[g, b * 128 : (b + 1) * 128, p * 128 : (p + 1) * 128]
                weights, tops = [], []
                for e in range(2):
                    far = lax.dot_general(q, kp[e, :SINK_TOK, :], contract_last, preferred_element_type=F32)
                    near = lax.dot_general(
                        q,
                        kp[e, SINK_TOK + b * 128 : SINK_TOK + b * 128 + 256, :],
                        contract_last,
                        preferred_element_type=F32,
                    )
                    before = near[:, :128]
                    if special:
                        index = lin * 4 + b
                        before = jnp.where(index > 0, before, NEG)
                        far = jnp.concatenate(
                            [
                                jnp.where(
                                    col - row <= 128 * (index - 1 - s), far[:, s * 128 : (s + 1) * 128], NEG
                                )
                                for s in range(4)
                            ],
                            axis=1,
                        )
                    close = jnp.where(own, near[:, 128:], before)
                    top = jnp.maximum(
                        jnp.maximum(
                            jnp.maximum(far[:, 0:128], far[:, 128:256]),
                            jnp.maximum(far[:, 256:384], far[:, 384:512]),
                        ),
                        close,
                    )
                    top = jnp.max(top, axis=1, keepdims=True)
                    top = jnp.maximum(top, sink_ref[g * 8 + 2 * p + e] * 8.0)
                    far_w = jnp.exp2((far - top) * EXP_SCALE).astype(BF16)
                    close_w = jnp.exp2((close - top) * EXP_SCALE)
                    before_w = jnp.where(own, 0.0, close_w).astype(BF16)
                    own_w = jnp.where(own, close_w, 0.0).astype(BF16)
                    weights.append((far_w, jnp.concatenate([before_w, own_w], axis=1)))
                    tops.append(top)
                acc = None
                for e in range(2):
                    one = jnp.broadcast_to(ones[e], (SINK_TOK, 128))
                    far_v = jnp.concatenate([vp[e, :SINK_TOK, :], one], axis=1)
                    near_v = jnp.concatenate(
                        [vp[e, SINK_TOK + b * 128 : SINK_TOK + b * 128 + 256, :], one[:256]], axis=1
                    )
                    part = jnp.dot(weights[e][0], far_v, preferred_element_type=F32)
                    part = part + jnp.dot(weights[e][1], near_v, preferred_element_type=F32)
                    acc = part if acc is None else acc + part
                top = jnp.where(low, tops[0], tops[1])
                sink = jnp.where(low, sink_ref[g * 8 + 2 * p], sink_ref[g * 8 + 2 * p + 1]) * 8.0
                sink_w = jnp.exp2((sink - top) * EXP_SCALE)
                inverse = 1.0 / (acc[:, 128:] + sink_w)
                ob[g, b * 128 : (b + 1) * 128, p * 128 : (p + 1) * 128] = (acc[:, :128] * inverse).astype(BF16)
                share[p] = share[p] + jnp.sum(sink_w * inverse, axis=0, keepdims=True)
        sh_ref[g] = jnp.concatenate(share, axis=0)
        cols = pl.ds(pl.multiple_of(g * 512, 512), 512)
        pltpu.make_async_copy(ob.at[g], o_hbm.at[:, cols], so.at[g]).start()

    @pl.when(lin < 2)
    def _():
        @pl.loop(0, 8)
        def _(g):
            group(g, True)

    @pl.when(lin >= 2)
    def _():
        @pl.loop(0, 8)
        def _(g):
            group(g, False)

    for g in range(8):
        pltpu.make_async_copy(ob.at[g], o_hbm.at[:, pl.ds(g * 512, 512)], so.at[g]).wait()


def attend(sink_logits, queries, kv, edge, keys, values):
    vmem = pl.BlockSpec(memory_space=pltpu.VMEM)
    hbm = pl.BlockSpec(memory_space=pl.ANY)
    return pl.pallas_call(
        attend_kernel,
        in_specs=[pl.BlockSpec(memory_space=pltpu.SMEM), hbm, vmem, vmem, vmem, vmem],
        out_specs=[hbm, vmem],
        out_shape=[
            jax.ShapeDtypeStruct((512, 4096), BF16),
            jax.ShapeDtypeStruct((8, 4, 128), F32),
        ],
        scratch_shapes=[
            pltpu.VMEM((8, 512, 512), BF16),
            pltpu.VMEM((8, 512, 512), BF16),
            pltpu.VMEM((2, 1152, 128), BF16),
            pltpu.VMEM((2, 1152, 128), BF16),
            pltpu.SemaphoreType.DMA((8,)),
            pltpu.SemaphoreType.DMA((8,)),
        ],
        compiler_params=pltpu.CompilerParams(vmem_limit_bytes=48 << 20),
    )(sink_logits, queries, kv, edge, keys, values)


def total_kernel(sh_ref, o_ref, one, two, s1, r1, s2, r2):
    z, x, y, c, lin = where_am_i()
    xy = 4 * x + y
    zc = 2 * z + c
    barrier = pltpu.get_barrier_semaphore()

    def other(step):
        at = lax.rem(zc + step, 16)
        return (at // 2, x, y, lax.rem(at, 2))

    for step in range(1, 16):
        signal(barrier, plane_peer(z, x, y, c, step))
        signal(barrier, other(step))
    row = lax.broadcasted_iota(jnp.int32, (32, 128), 0)
    lane = lax.broadcasted_iota(jnp.int32, (32, 128), 1)
    a = sh_ref[...]
    mine = jnp.sum(
        jnp.where(lane == 2 * row, a, 0.0) + jnp.where(lane == 2 * row + 1, pltpu.roll(a, 64, 1), 0.0),
        axis=0,
        keepdims=True,
    )
    one[xy] = jnp.broadcast_to(mine, (8, 128))
    pl.semaphore_wait(barrier, 30)

    def exchange(buf, at, peer, send, recv):
        for step in range(1, 16):
            pltpu.make_async_remote_copy(
                buf.at[at], buf.at[at], send, recv, device_id=peer(step), device_id_type=MESH
            ).start()
        many = buf.at[pl.ds(0, 15)]
        copy = pltpu.make_async_remote_copy(many, many, send, recv, device_id=(z, x, y, c), device_id_type=MESH)
        copy.wait_recv()
        return copy

    plane = functools.partial(plane_peer, z, x, y, c)
    first = exchange(one, xy, plane, s1, r1)
    two[zc] = jnp.sum(one[...], axis=0)
    second = exchange(two, zc, other, s2, r2)
    o_ref[...] = jnp.sum(two[...], axis=0) * (1.0 / 131072)
    first.wait_send()
    second.wait_send()


def total(shares):
    vmem = pl.BlockSpec(memory_space=pltpu.VMEM)
    dma = pltpu.SemaphoreType.DMA
    return pl.pallas_call(
        total_kernel,
        in_specs=[vmem],
        out_specs=vmem,
        out_shape=jax.ShapeDtypeStruct((8, 128), F32),
        scratch_shapes=[pltpu.VMEM((16, 8, 128), F32)] * 2 + [dma(())] * 4,
        compiler_params=pltpu.CompilerParams(collective_id=1, has_side_effects=True),
    )(shares.reshape(32, 128))


def local(queries, keys, values, sink_logits):
    kv, edge = spread(keys, values)
    attended, shares = attend(sink_logits, queries, kv, edge, keys, values)
    return attended, total(shares)[0, :64]


def solution(mesh):
    torus = Mesh(mesh.devices.reshape(SIZES), AXES)
    rows = P(AXES, None)
    return jax.shard_map(
        local, mesh=torus, in_specs=(rows, rows, rows, P()), out_specs=(rows, P()), check_vma=False
    )
```

time: 532 us -> 93.5 us (0.18)
  other arithmetic: 119 us -> 0 us
  starting transfers between devices: 116 us -> 0 us
  blocking collectives: 111 us -> 0 us
  matrix products: 87.8 us -> 0 us
  Pallas kernels: 0 us -> 85.8 us
  local copies, waits for them, and re-layouts: 59.5 us -> 6.69 us
  waiting for transfers between devices: 33.3 us -> 0 us
    ppermute x18 -> x0, starting transfers between devices: 116 us -> none  [from_behind(): return lax.ppermute(block, axis, route)]
    psum x4 -> x0, blocking collectives: 111 us -> none  [one_axis_at_a_time(): return functools.reduce(lax.psum, axes, x)]
    dot_general x32 -> x0, matrix products: 87.8 us -> none  [the longest x8 42.7 us: per_head(): jnp.einsum('btgd,sd->gbts', query_part, sink_kpart, preferred_element_typ...]
    pallas_call x0 -> x3, Pallas kernels: none -> 85.8 us  [the longest x1 37.2 us: attend(): pl.pallas_call(attend_kernel, in_specs=[pl.BlockSpec(memory_space=pltpu.S...]
    reduce_sum x16 -> x0, other arithmetic: 53.9 us -> none  [the longest x8 52.4 us: per_head(): total = jnp.sum(weight, axis=-1) + sink_weight]
    reduce_max x8 -> x0, other arithmetic: 49.3 us -> none  [per_head(): row_max = jnp.maximum(jnp.max(scores, axis=-1), sink_part[:, None, None])]
    ppermute x18 -> x0, waiting for transfers between devices: 33.3 us -> none  [from_behind(): return lax.ppermute(block, axis, route)]
    unnamed x11 -> x12, local copies, waits for them, and re-layouts: 32.8 us -> 5.5 us
  transfers between devices with their start and end apart: 18 -> 0, of which waited for: 8 -> 0; matrix products, arithmetic and copies ran while one was open for 7% -> 0% of each run, Pallas kernels for 0% -> 0%
where the time goes in v1:
time: 93.5 us; the launch traced here: 93.2 us
  Pallas kernels  85.8 us (92%)
  local copies, waits for them, and re-layouts  6.69 us (7%)
    pallas_call x1, Pallas kernels, attend(): pl.pallas_call(attend_kernel, in_specs=[pl.BlockSpec(memory_space=pltpu.S...  37.2 us
    pallas_call x1, Pallas kernels, spread(): pl.pallas_call(spread_kernel, in_specs=[pl.BlockSpec(memory_space=pl.ANY)...  30.6 us
    pallas_call x1, Pallas kernels, total(): pl.pallas_call(total_kernel, in_specs=[vmem], out_specs=vmem, out_shape=j...  18 us
    unnamed x12, local copies, waits for them, and re-layouts  5.5 us

profile of v1, /device:TPU:1, one launch (start us, length us, event | category | flops | bytes accessed | tf_op | source)
XLA Modules:
  0.0 93.2 jit_solution(17010040661388467036)
XLA Ops:
  0.6 30.6 %shard_map.59 = (bf16[2,512,512]{2,1,0:T(8,128)(2,1)}, bf16[2,128,512]{2,1,0:T(8,128)(2,1)}) custom-call(bf16[512,512]{1,0:T(8,128)(2,1)} %k_ref.3, bf16[512,512]{1,0:T(8,128)(2,1)} %v_ref.3), custom_call_target="tpu_custom_call" | custom-call | tf_op jit(solution)/shard_map/pallas_call | solution.py:139
  31.2 0.0 copy-start
  31.2 1.0 %copy-done = bf16[512,512]{1,0:T(8,128)(2,1)S(1)} copy-done((bf16[512,512]{1,0:T(8,128)(2,1)S(1)}, bf16[512,512]{1,0:T(8,128)(2,1)}, u32[]{:S(2)}) %copy-start) | copy-done | bytes 524312
  32.3 0.0 copy-start.1
  32.3 1.0 %copy-done.1 = bf16[512,512]{1,0:T(8,128)(2,1)S(1)} copy-done((bf16[512,512]{1,0:T(8,128)(2,1)S(1)}, bf16[512,512]{1,0:T(8,128)(2,1)}, u32[]{:S(2)}) %copy-start.1) | copy-done | bytes 524312
  33.3 0.0 copy-start.2
  33.3 1.2 %copy-done.2 = bf16[2,512,512]{2,1,0:T(8,128)(2,1)S(1)} copy-done((bf16[2,512,512]{2,1,0:T(8,128)(2,1)S(1)}, bf16[2,512,512]{2,1,0:T(8,128)(2,1)}, u32[]{:S(2)}) %copy-start.2) | copy-done | bytes 1048600
  34.5 0.0 copy-start.3
  34.5 0.9 %copy-done.3 = bf16[2,128,512]{2,1,0:T(8,128)(2,1)S(1)} copy-done((bf16[2,128,512]{2,1,0:T(8,128)(2,1)S(1)}, bf16[2,128,512]{2,1,0:T(8,128)(2,1)}, u32[]{:S(2)}) %copy-start.3) | copy-done | bytes 262168
  35.5 0.0 copy-start.5
  35.5 0.7 copy-done.5
  36.2 37.2 %shard_map.60 = (bf16[512,4096]{1,0:T(8,128)(2,1)}, f32[8,4,128]{2,1,0:T(4,128)S(1)}) custom-call(f32[64]{0:T(128)S(1)} %copy-done.5, bf16[512,4096]{1,0:T(8,128)(2,1)} %q_hbm.1, bf16[2,512,512]{2,1,0:T(8,128)(2,1)S(1)} %copy-done.2, bf16[2,128,512]{2,1,0:T(8,128)(2,1)S(1)} %copy-done.3, bf16[512,512]{1,0:T(8,128)(2,1)S(1)} %copy-done, ...), custom_call_target="tpu_custom_call" | custom-call | tf_op jit(solution)/shard_map/pallas_call | solution.py:281
  73.3 0.0 copy-start.4
  73.3 0.6 copy-done.4
  73.9 18.0 %shard_map.61 = f32[8,128]{1,0:T(8,128)} custom-call(f32[32,128]{1,0:T(8,128)} %bitcast.3), custom_call_target="tpu_custom_call" | custom-call | tf_op jit(solution)/shard_map/pallas_call | solution.py:347
  92.0 1.2 %slice_bitcast_fusion = f32[64]{0:T(128)} fusion(f32[8,128]{1,0:T(8,128)} %shard_map.61), kind=kLoop, calls=%fused_computation | loop fusion | bytes 512 | tf_op jit(solution)/shard_map/squeeze | solution.py:360
Async XLA Ops:
  31.2 1.0 %copy-start = (bf16[512,512]{1,0:T(8,128)(2,1)S(1)}, bf16[512,512]{1,0:T(8,128)(2,1)}, u32[]{:S(2)}) copy-start(bf16[512,512]{1,0:T(8,128)(2,1)} %k_ref.3) | copy-start | bytes 1572868
  32.3 1.0 %copy-start.1 = (bf16[512,512]{1,0:T(8,128)(2,1)S(1)}, bf16[512,512]{1,0:T(8,128)(2,1)}, u32[]{:S(2)}) copy-start(bf16[512,512]{1,0:T(8,128)(2,1)} %v_ref.3) | copy-start | bytes 1572868
  33.3 1.2 %copy-start.2 = (bf16[2,512,512]{2,1,0:T(8,128)(2,1)S(1)}, bf16[2,512,512]{2,1,0:T(8,128)(2,1)}, u32[]{:S(2)}) copy-start(bf16[2,512,512]{2,1,0:T(8,128)(2,1)} %get-tuple-element.6.kv_ref) | copy-start | bytes 3145732
  34.5 0.9 %copy-start.3 = (bf16[2,128,512]{2,1,0:T(8,128)(2,1)S(1)}, bf16[2,128,512]{2,1,0:T(8,128)(2,1)}, u32[]{:S(2)}) copy-start(bf16[2,128,512]{2,1,0:T(8,128)(2,1)} %get-tuple-element.7.edge_ref) | copy-start | bytes 786436
  35.5 0.7 copy-start.5
  73.3 0.6 copy-start.4

commit v2 on v0

v2 whole, which is shorter than its diff:
```python
import functools

import jax
import jax.numpy as jnp
from jax import lax
from jax.experimental import pallas as pl
from jax.experimental.pallas import tpu as pltpu
from jax.sharding import Mesh
from jax.sharding import PartitionSpec as P

WINDOW = 128
SINK_TOK = 512
AXES = ("seq_0", "seq_1", "seq_2", "seq_3")
SIZES = (8, 4, 4, 2)
MESH = pl.DeviceIdType.MESH
F32 = jnp.float32
BF16 = jnp.bfloat16
NEG = -1e30
LOG2E = 1.4426950408889634
PIECE = 32
LATE = 4
EARLY = 8 - LATE
NT = (((1,), (1,)), ((), ()))


def signal(sem, device):
    pl.semaphore_signal(sem, inc=1, device_id=device, device_id_type=MESH)


def coords(lin):
    return (lin // 32, lax.rem(lin // 8, 4), lax.rem(lin // 2, 4), lax.rem(lin, 2))


def padded_keys(tile):
    low = lax.broadcasted_iota(jnp.int32, tile.shape, 1) < 64
    wide = tile.astype(F32) * (LOG2E / 8.0)
    high_term = wide.astype(BF16).astype(F32)
    low_term = wide - high_term
    out = []
    for half in range(2):
        here, moved = [], []
        for term in (high_term, low_term):
            alone = jnp.where(low, term, 0.0) if half == 0 else jnp.where(low, 0.0, term)
            here.append(alone.astype(BF16))
            moved.append(pltpu.roll(alone, 64, 1).astype(BF16))
        here = jnp.concatenate(here, axis=1)
        moved = jnp.concatenate(moved, axis=1)
        out.append((here, moved) if half == 0 else (moved, here))
    return out


def fold(x, op):
    parts = [x[i : i + 8] for i in range(0, x.shape[0], 8)]
    while len(parts) > 1:
        parts = [op(parts[i], parts[i + 1]) for i in range(0, len(parts), 2)]
    return parts[0]


def across(x, op):
    for shift in (4, 2, 1):
        x = op(x, pltpu.roll(x, shift, 0))
    return x


def tall(x, n):
    return jnp.concatenate([x] * n, axis=0)


def kernel(
    sink_ref, q_hbm, k_hbm, v_hbm, o_ref, total_ref,
    qb, kx, vx, kv, kpw, kps, vtw, vts, ow, mw, lw, sb, tb, pb, rb, late_p, late_r, sh, one, two,
    sq, sk, s1, r1, s2, r2, s3, r3, s4, r4, se, re, s5, r5, s6, r6,
):
    z, x, y, c = (lax.axis_index(a) for a in AXES)
    lin = ((z * 4 + x) * 4 + y) * 2 + c
    xy = 4 * x + y
    zc = 2 * z + c
    first = lin == 0
    relay = z == 0
    me = (z, x, y, c)
    rows = pl.ds(pl.multiple_of(xy * PIECE, PIECE), PIECE)

    def plane(step):
        return (z, lax.rem(x + step // 4, 4), lax.rem(y + step % 4, 4), c)

    def column(step):
        at = lax.rem(zc + step, 16)
        return (at // 2, x, y, lax.rem(at, 2))

    def remote(src, dst, send, recv, device):
        return pltpu.make_async_remote_copy(
            src_ref=src, dst_ref=dst, send_sem=send, recv_sem=recv, device_id=device, device_id_type=MESH
        )

    loads = [
        pltpu.make_async_copy(k_hbm, kx.at[pl.ds(WINDOW, 512)], sk.at[0]),
        pltpu.make_async_copy(v_hbm, vx.at[pl.ds(WINDOW, 512)], sk.at[1]),
    ]
    q_load = pltpu.make_async_copy(q_hbm, qb, sq)
    for copy in loads:
        copy.start()
    q_load.start()

    barrier = pltpu.get_barrier_semaphore()

    @pl.when(relay & (lin > 0))
    def _():
        signal(barrier, (0, 0, 0, 0))

    @pl.when(lin > 0)
    def _():
        signal(barrier, coords(lin - 1))

    for step in range(1, 16):
        signal(barrier, plane(step))
        signal(barrier, column(step))

    pl.semaphore_wait(barrier, 30 + jnp.where(lin < 255, 1, 0) + jnp.where(first, 31, 0))
    for copy in loads:
        copy.wait()

    @pl.when(first)
    def _():
        for p in range(16):
            for cc, ref in ((0, kx), (1, vx)):
                src = ref.at[pl.ds(WINDOW + p * PIECE, PIECE)]
                dst = kv.at[cc, pl.ds(p * PIECE, PIECE)]
                if cc == 0 and p == 0:
                    pltpu.make_async_copy(src, dst, r1).start()
                else:
                    remote(src, dst, s1, r1, (0, p // 4, p % 4, cc)).start()
        for i, ref in enumerate((kx, vx)):
            ref[pl.ds(0, WINDOW), :] = jnp.zeros((WINDOW, 512), BF16)

    @pl.when(lin < 255)
    def _():
        for i, ref in enumerate((kx, vx)):
            remote(ref.at[pl.ds(512, WINDOW)], ref.at[pl.ds(0, WINDOW)], se.at[i], re.at[i], coords(lin + 1)).start()

    def prepare(kp, vt, keys, values, start, size, src):
        for pair in range(4):
            cols = pl.ds(pair * 128, 128)
            made = padded_keys(keys[pl.ds(src, size), cols])
            turned = values[pl.ds(src, size), cols].T.reshape(2, 64, size)
            for half in range(2):
                g = 2 * pair + half
                for e in range(2):
                    kp[g, e, start : start + size, :] = made[half][e]
                vt[g, 0:64, start : start + size] = turned[half]

    vtw[:, 64:80, :] = jnp.ones((8, 16, 640), BF16)
    vts[:, 64:80, :] = jnp.ones((8, 16, 512), BF16)
    prepare(kpw, vtw, kx, vx, WINDOW, 512, WINDOW)

    row = lax.broadcasted_iota(jnp.int32, (128, 512), 0)
    col = lax.rem(lax.broadcasted_iota(jnp.int32, (128, 512), 1), 128)
    own = row <= col
    which = lax.broadcasted_iota(jnp.int32, (8, 512), 1) // 128

    def q_tile(g, b):
        cols = [
            qb[b * 128 : b * 128 + 128, pl.ds(pl.multiple_of(g * 512 + p * 128, 128), 128)] for p in range(4)
        ]
        tile = jnp.concatenate(cols, axis=0)
        return jnp.concatenate([tile, tile], axis=1)

    def sink_row(g, e):
        out = jnp.full((8, 512), sink_ref[g * 8 + e] * LOG2E, F32)
        for p in range(1, 4):
            out = jnp.where(which == p, sink_ref[g * 8 + 2 * p + e] * LOG2E, out)
        return out

    def near_scores(g, b, slot):
        start = b * 128
        both = jnp.concatenate([kpw[g, e, start : start + 256, :] for e in range(2)], axis=0)
        s = lax.dot_general(both, q_tile(g, b), NT, preferred_element_type=F32)
        for e in range(2):
            before = s[e * 256 : e * 256 + 128]
            if b == 0:
                before = jnp.where(first, NEG, before)
            w = jnp.where(own, s[e * 256 + 128 : e * 256 + 256], before)
            sb[slot, e, :128] = w
            tb[slot, e] = fold(w, jnp.maximum)

    def near_weights(g, b, slot):
        for e in range(2):
            sink = sink_row(g, e)
            top = jnp.maximum(across(tb[slot, e], jnp.maximum), sink)
            w = jnp.exp2(sb[slot, e, :128] - tall(top, 16))
            pb[slot, e, :128] = jnp.where(own, 0.0, w).astype(BF16)
            pb[slot, e, 128:256] = jnp.where(own, w, 0.0).astype(BF16)
            mw[g, b, e] = top
            rb[slot, e, 0] = jnp.exp2(sink - top)

    def near_values(g, b, slot):
        for e in range(2):
            o = jnp.dot(vtw[g, :, b * 128 : b * 128 + 256], pb[slot, e, :256], preferred_element_type=F32)
            ow[g, b, e] = o[:64]
            lw[g, b, e] = rb[slot, e, 0] + o[64:72]

    def near_pass(blocks):
        units = [(h, b) for h in range(2) for b in blocks]
        n = len(units)
        near_scores(0, blocks[0], 0)

        @pl.loop(0, 4)
        def _(pair):
            for u, (h, b) in enumerate(units):
                slot = u % 2
                if u + 1 < n:
                    near_scores(2 * pair + units[u + 1][0], units[u + 1][1], 1 - slot)
                else:
                    near_scores(jnp.minimum(2 * pair + 2, 6), blocks[0], 1 - slot)
                if u > 0:
                    near_values(2 * pair + units[u - 1][0], units[u - 1][1], 1 - slot)
                else:
                    near_values(jnp.maximum(2 * pair - 1, 0), units[n - 1][1], 1 - slot)
                near_weights(2 * pair + h, b, slot)

        near_values(7, blocks[-1], 1)

    piece = kv.at[c, rows]

    def spread_plane():
        for step in range(1, 16):
            remote(piece, piece, s3, r3, plane(step)).start()

    q_load.wait()
    pb[...] = jnp.zeros_like(pb)
    rb[...] = jnp.zeros_like(rb)
    near_pass((3, 2))

    @pl.when(relay)
    def _():
        remote(piece, piece, s2, r1, me).wait_recv()
        for zz in range(1, 8):
            remote(piece, piece, s2, r2, (zz, x, y, c)).start()
        spread_plane()

    near_pass((1,))

    @pl.when(z > 0)
    def _():
        remote(piece, piece, s2, r2, me).wait_recv()
        spread_plane()

    @pl.when(lin > 0)
    def _():
        for i, ref in enumerate((kx, vx)):
            remote(ref.at[pl.ds(512, WINDOW)], ref.at[pl.ds(0, WINDOW)], se.at[i], re.at[i], me).wait_recv()

    prepare(kpw, vtw, kx, vx, 0, WINDOW, 0)
    near_pass((0,))

    fifteen = kv.at[c, pl.ds(0, 15 * PIECE)]
    remote(fifteen, fifteen, s3, r3, me).wait_recv()
    half = remote(kv.at[c], kv.at[c], s4, r4, (z, x, y, 1 - c))
    half.start()
    half.wait_recv()
    prepare(kps, vts, kv.at[0], kv.at[1], 0, 512, 0)

    def far_scores(g, b, slot, special):
        both = jnp.concatenate([kps[g, e] for e in range(2)], axis=0)
        s = lax.dot_general(both, q_tile(g, b), NT, preferred_element_type=F32)
        for e in range(2):
            part = s[e * 512 : e * 512 + 512]
            if special:
                index = lin * 4 + b
                part = jnp.concatenate(
                    [
                        jnp.where(row - col <= 128 * (index - 1 - i), part[i * 128 : i * 128 + 128], NEG)
                        for i in range(4)
                    ],
                    axis=0,
                )
            sb[slot, e] = part
            tb[slot, e] = fold(part, jnp.maximum)

    def far_weights(g, b, slot, late):
        for e in range(2):
            old = mw[g, b, e]
            top = jnp.maximum(across(tb[slot, e], jnp.maximum), old)
            scale = jnp.exp2(old - top)
            sink = jnp.exp2(sink_row(g, e) - top)
            dst = late_p.at[(g - EARLY) * 4 + b, e] if late else pb.at[slot, e]
            acc = None
            for r in range(0, 512, 64):
                w = jnp.exp2(sb[slot, e, r : r + 64] - tall(top, 8))
                dst[r : r + 64, :] = w.astype(BF16)
                if late:
                    part = fold(w, jnp.add)
                    acc = part if acc is None else acc + part
            if late:
                inverse = 1.0 / (lw[g, b, e] * scale + across(acc, jnp.add))
                sh[g, e] += sink * inverse
                late_r[(g - EARLY) * 4 + b, e, 0] = scale * inverse
                late_r[(g - EARLY) * 4 + b, e, 1] = inverse
            else:
                rb[slot, e, 0] = scale
                rb[slot, e, 1] = sink

    def put(g, b, outs):
        both = jnp.concatenate(outs, axis=0)
        for p in range(4):
            cols = pl.ds(pl.multiple_of(g * 512 + p * 128, 128), 128)
            o_ref[b * 128 : b * 128 + 128, cols] = both[:, p * 128 : p * 128 + 128].T

    def far_values(g, b, slot, share_at):
        outs = []
        for e in range(2):
            o = jnp.dot(vts[g], pb[slot, e], preferred_element_type=F32)
            scale = rb[slot, e, 0]
            inverse = 1.0 / (lw[g, b, e] * scale + o[64:72])
            sh[share_at, e] += rb[slot, e, 1] * inverse
            outs.append((o[:64] * tall(inverse, 8) + ow[g, b, e] * tall(scale * inverse, 8)).astype(BF16))
        put(g, b, outs)

    def late_values(g, b):
        outs = []
        at = (g - EARLY) * 4 + b
        for e in range(2):
            o = jnp.dot(vts[g, 0:64, :], late_p[at, e], preferred_element_type=F32)
            outs.append((o * tall(late_r[at, e, 1], 8) + ow[g, b, e] * tall(late_r[at, e, 0], 8)).astype(BF16))
        put(g, b, outs)

    sh[...] = jnp.zeros_like(sh)

    def far_pass(special):
        far_scores(0, 0, 0, special)

        @pl.loop(0, EARLY)
        def _(g):
            for b in range(4):
                slot = b % 2
                if b < 3:
                    far_scores(g, b + 1, 1 - slot, special)
                else:
                    far_scores(g + 1, 0, 1 - slot, special)
                if b > 0:
                    far_values(g, b - 1, 1 - slot, g)
                else:
                    far_values(jnp.maximum(g - 1, 0), 3, 1 - slot, jnp.where(g > 0, g - 1, 8))
                far_weights(g, b, slot, False)

        far_values(EARLY - 1, 3, 1, EARLY - 1)

        @pl.loop(EARLY, 8)
        def _(g):
            for b in range(4):
                slot = b % 2
                if b < 3:
                    far_scores(g, b + 1, 1 - slot, special)
                else:
                    far_scores(jnp.minimum(g + 1, 7), 0, 1 - slot, special)
                far_weights(g, b, slot, True)

    @pl.when(lin < 2)
    def _():
        far_pass(True)

    @pl.when(lin >= 2)
    def _():
        far_pass(False)

    lane = lax.broadcasted_iota(jnp.int32, (8, 128), 1)
    mine = jnp.zeros((8, 128), F32)
    for g in range(8):
        for e in range(2):
            for p in range(4):
                part = jnp.sum(sh[g, e, :, p * 128 : p * 128 + 128], axis=1, keepdims=True)
                mine = jnp.where(lane == g * 8 + 2 * p + e, part, mine)
    one[xy] = mine
    for step in range(1, 16):
        remote(one.at[xy], one.at[xy], s5, r5, plane(step)).start()

    @pl.loop(EARLY, EARLY + LATE // 2)
    def _(g):
        for b in range(4):
            late_values(g, b)

    many = one.at[pl.ds(0, 15)]
    remote(many, many, s5, r5, me).wait_recv()
    two[zc] = jnp.sum(one[...], axis=0)
    for step in range(1, 16):
        remote(two.at[zc], two.at[zc], s6, r6, column(step)).start()

    @pl.loop(EARLY + LATE // 2, 8)
    def _(g):
        for b in range(4):
            late_values(g, b)

    lots = two.at[pl.ds(0, 15)]
    remote(lots, lots, s6, r6, me).wait_recv()
    total_ref[...] = jnp.sum(two[...], axis=0) * (1.0 / 131072)

    remote(many, many, s5, r5, me).wait_send()
    remote(lots, lots, s6, r6, me).wait_send()
    half.wait_send()
    remote(fifteen, fifteen, s3, r3, me).wait_send()

    @pl.when(relay)
    def _():
        seven = kv.at[c, pl.ds(0, 7 * PIECE)]
        remote(seven, seven, s2, r2, me).wait_send()

    @pl.when(first)
    def _():
        sent = kv.at[:, pl.ds(0, 496)]
        remote(sent, sent, s1, r1, me).wait_send()

    @pl.when(lin < 255)
    def _():
        for i, ref in enumerate((kx, vx)):
            remote(ref.at[pl.ds(512, WINDOW)], ref.at[pl.ds(0, WINDOW)], se.at[i], re.at[i], me).wait_send()


def local(queries, keys, values, sink_logits):
    vmem = pl.BlockSpec(memory_space=pltpu.VMEM)
    hbm = pl.BlockSpec(memory_space=pl.ANY)
    dma = pltpu.SemaphoreType.DMA
    attended, total = pl.pallas_call(
        kernel,
        in_specs=[pl.BlockSpec(memory_space=pltpu.SMEM), hbm, hbm, hbm],
        out_specs=[vmem, vmem],
        out_shape=[jax.ShapeDtypeStruct((512, 4096), BF16), jax.ShapeDtypeStruct((8, 128), F32)],
        scratch_shapes=[
            pltpu.VMEM((512, 4096), BF16),
            pltpu.VMEM((640, 512), BF16),
            pltpu.VMEM((640, 512), BF16),
            pltpu.VMEM((2, 512, 512), BF16),
            pltpu.VMEM((8, 2, 640, 256), BF16),
            pltpu.VMEM((8, 2, 512, 256), BF16),
            pltpu.VMEM((8, 80, 640), BF16),
            pltpu.VMEM((8, 80, 512), BF16),
            pltpu.VMEM((8, 4, 2, 64, 512), F32),
            pltpu.VMEM((8, 4, 2, 8, 512), F32),
            pltpu.VMEM((8, 4, 2, 8, 512), F32),
            pltpu.VMEM((2, 2, 512, 512), F32),
            pltpu.VMEM((2, 2, 8, 512), F32),
            pltpu.VMEM((2, 2, 512, 512), BF16),
            pltpu.VMEM((2, 2, 2, 8, 512), F32),
            pltpu.VMEM((LATE * 4, 2, 512, 512), BF16),
            pltpu.VMEM((LATE * 4, 2, 2, 8, 512), F32),
            pltpu.VMEM((9, 2, 8, 512), F32),
            pltpu.VMEM((16, 8, 128), F32),
            pltpu.VMEM((16, 8, 128), F32),
            dma(()),
            dma((2,)),
        ]
        + [dma(())] * 8
        + [dma((2,))] * 2
        + [dma(())] * 4,
        compiler_params=pltpu.CompilerParams(
            collective_id=0, has_side_effects=True, vmem_limit_bytes=60 << 20
        ),
    )(sink_logits, queries, keys, values)
    return attended, total[0, :64]


def solution(mesh):
    torus = Mesh(mesh.devices.reshape(SIZES), AXES)
    rows = P(AXES, None)
    return jax.shard_map(
        local, mesh=torus, in_specs=(rows, rows, rows, P()), out_specs=(rows, P()), check_vma=False
    )
```

time: 532 us -> 74.3 us (0.14)
  other arithmetic: 119 us -> 0 us
  starting transfers between devices: 116 us -> 0 us
  blocking collectives: 111 us -> 0 us
  matrix products: 87.8 us -> 0 us
  Pallas kernels: 0 us -> 67.6 us
  local copies, waits for them, and re-layouts: 59.5 us -> 5.88 us
  waiting for transfers between devices: 33.3 us -> 0 us
    ppermute x18 -> x0, starting transfers between devices: 116 us -> none  [from_behind(): return lax.ppermute(block, axis, route)]
    psum x4 -> x0, blocking collectives: 111 us -> none  [one_axis_at_a_time(): return functools.reduce(lax.psum, axes, x)]
    dot_general x32 -> x0, matrix products: 87.8 us -> none  [the longest x8 42.7 us: per_head(): jnp.einsum('btgd,sd->gbts', query_part, sink_kpart, preferred_element_typ...]
    pallas_call x0 -> x1, Pallas kernels: none -> 67.6 us  [local(): pl.pallas_call(kernel, in_specs=[pl.BlockSpec(memory_space=pltpu.SMEM), h...]
    reduce_sum x16 -> x0, other arithmetic: 53.9 us -> none  [the longest x8 52.4 us: per_head(): total = jnp.sum(weight, axis=-1) + sink_weight]
    reduce_max x8 -> x0, other arithmetic: 49.3 us -> none  [per_head(): row_max = jnp.maximum(jnp.max(scores, axis=-1), sink_part[:, None, None])]
    ppermute x18 -> x0, waiting for transfers between devices: 33.3 us -> none  [from_behind(): return lax.ppermute(block, axis, route)]
    unnamed x11 -> x1, local copies, waits for them, and re-layouts: 32.8 us -> 4.7 us
  transfers between devices with their start and end apart: 18 -> 0, of which waited for: 8 -> 0; matrix products, arithmetic and copies ran while one was open for 7% -> 0% of each run, Pallas kernels for 0% -> 0%
where the time goes in v2:
time: 74.3 us; the launch traced here: 74.1 us
  Pallas kernels  67.6 us (91%)
  local copies, waits for them, and re-layouts  5.88 us (8%)
    pallas_call x1, Pallas kernels, local(): pl.pallas_call(kernel, in_specs=[pl.BlockSpec(memory_space=pltpu.SMEM), h...  67.6 us
    unnamed x1, local copies, waits for them, and re-layouts  4.7 us

profile of v2, /device:TPU:1, one launch (start us, length us, event | category | flops | bytes accessed | tf_op | source)
XLA Modules:
  0.0 74.1 jit_solution(16644005492120946567)
XLA Ops:
  0.6 67.6 %shard_map.59 = (bf16[512,4096]{1,0:T(8,128)(2,1)}, f32[8,128]{1,0:T(8,128)}) custom-call(f32[64]{0:T(128)} %sink_ref.1, bf16[512,4096]{1,0:T(8,128)(2,1)} %q_hbm.1, bf16[512,512]{1,0:T(8,128)(2,1)} %k_hbm.1, bf16[512,512]{1,0:T(8,128)(2,1)} %v_hbm.1), custom_call_target="tpu_custom_call" | custom-call | tf_op jit(solution)/shard_map/pallas_call | solution.py:421
  68.3 1.2 %slice_bitcast_fusion = f32[64]{0:T(128)} fusion(f32[8,128]{1,0:T(8,128)} %get-tuple-element.5), kind=kLoop, calls=%fused_computation | loop fusion | bytes 512 | tf_op jit(solution)/shard_map/squeeze | solution.py:457
  69.5 4.7 %copy.7 = bf16[512,4096]{1,0:T(8,128)(2,1)} copy(bf16[512,4096]{1,0:T(8,128)(2,1)} %get-tuple-element.8) | data formatting | bytes 8388608

commit v3 on v2

--- a/solution.py
+++ b/solution.py
@@ -52,7 +52,8 @@
 def fold(x, op):
     parts = [x[i : i + 8] for i in range(0, x.shape[0], 8)]
     while len(parts) > 1:
-        parts = [op(parts[i], parts[i + 1]) for i in range(0, len(parts), 2)]
+        odd = parts[len(parts) // 2 * 2 :]
+        parts = [op(parts[i], parts[i + 1]) for i in range(0, len(parts) - 1, 2)] + odd
     return parts[0]
 
 
@@ -67,9 +68,9 @@
 
 
 def kernel(
-    sink_ref, q_hbm, k_hbm, v_hbm, o_ref, total_ref,
-    qb, kx, vx, kv, kpw, kps, vtw, vts, ow, mw, lw, sb, tb, pb, rb, late_p, late_r, sh, one, two,
-    sq, sk, s1, r1, s2, r2, s3, r3, s4, r4, se, re, s5, r5, s6, r6,
+    sink_ref, q_hbm, k_hbm, v_hbm, o_hbm, total_ref,
+    qb, ob, kx, vx, kv, kpw, kps, vtw, vts, ow, mw, lw, sb, tb, pb, rb, late_p, late_r, sh, one, two,
+    sq, sk, so, s1, r1, s2, r2, s3, r3, s4, r4, se, re, s5, r5, s6, r6,
 ):
     z, x, y, c = (lax.axis_index(a) for a in AXES)
     lin = ((z * 4 + x) * 4 + y) * 2 + c
@@ -79,6 +80,7 @@
     relay = z == 0
     me = (z, x, y, c)
     rows = pl.ds(pl.multiple_of(xy * PIECE, PIECE), PIECE)
+    cols = (pl.ds(0, 256), pl.ds(256, 256))
 
     def plane(step):
         return (z, lax.rem(x + step // 4, 4), lax.rem(y + step % 4, 4), c)
@@ -121,14 +123,15 @@
 
     @pl.when(first)
     def _():
-        for p in range(16):
-            for cc, ref in ((0, kx), (1, vx)):
-                src = ref.at[pl.ds(WINDOW + p * PIECE, PIECE)]
-                dst = kv.at[cc, pl.ds(p * PIECE, PIECE)]
-                if cc == 0 and p == 0:
-                    pltpu.make_async_copy(src, dst, r1).start()
-                else:
-                    remote(src, dst, s1, r1, (0, p // 4, p % 4, cc)).start()
+        for h in range(2):
+            for p in range(16):
+                for cc, ref in ((0, kx), (1, vx)):
+                    src = ref.at[pl.ds(WINDOW + p * PIECE, PIECE), cols[h]]
+                    dst = kv.at[cc, pl.ds(p * PIECE, PIECE), cols[h]]
+                    if cc == 0 and p == 0:
+                        pltpu.make_async_copy(src, dst, r1.at[h]).start()
+                    else:
+                        remote(src, dst, s1.at[h], r1.at[h], (0, p // 4, p % 4, cc)).start()
         for i, ref in enumerate((kx, vx)):
             ref[pl.ds(0, WINDOW), :] = jnp.zeros((WINDOW, 512), BF16)
 
@@ -137,11 +140,11 @@
         for i, ref in enumerate((kx, vx)):
             remote(ref.at[pl.ds(512, WINDOW)], ref.at[pl.ds(0, WINDOW)], se.at[i], re.at[i], coords(lin + 1)).start()
 
-    def prepare(kp, vt, keys, values, start, size, src):
-        for pair in range(4):
-            cols = pl.ds(pair * 128, 128)
-            made = padded_keys(keys[pl.ds(src, size), cols])
-            turned = values[pl.ds(src, size), cols].T.reshape(2, 64, size)
+    def prepare(kp, vt, keys, values, start, size, src, pairs=range(4)):
+        for pair in pairs:
+            lanes = pl.ds(pair * 128, 128)
+            made = padded_keys(keys[pl.ds(src, size), lanes])
+            turned = values[pl.ds(src, size), lanes].T.reshape(2, 64, size)
             for half in range(2):
                 g = 2 * pair + half
                 for e in range(2):
@@ -219,11 +222,11 @@
 
         near_values(7, blocks[-1], 1)
 
-    piece = kv.at[c, rows]
-
-    def spread_plane():
+    piece = [kv.at[c, rows, cols[h]] for h in range(2)]
+
+    def spread_plane(h):
         for step in range(1, 16):
-            remote(piece, piece, s3, r3, plane(step)).start()
+            remote(piece[h], piece[h], s3.at[h], r3.at[h], plane(step)).start()
 
     q_load.wait()
     pb[...] = jnp.zeros_like(pb)
@@ -232,17 +235,18 @@
 
     @pl.when(relay)
     def _():
-        remote(piece, piece, s2, r1, me).wait_recv()
-        for zz in range(1, 8):
-            remote(piece, piece, s2, r2, (zz, x, y, c)).start()
-        spread_plane()
+        for h in range(2):
+            remote(piece[h], piece[h], s2.at[h], r1.at[h], me).wait_recv()
+            for zz in range(1, 8):
+                remote(piece[h], piece[h], s2.at[h], r2.at[h], (zz, x, y, c)).start()
+            spread_plane(h)
 
     near_pass((1,))
 
     @pl.when(z > 0)
     def _():
-        remote(piece, piece, s2, r2, me).wait_recv()
-        spread_plane()
+        remote(piece[0], piece[0], s2.at[0], r2.at[0], me).wait_recv()
+        spread_plane(0)
 
     @pl.when(lin > 0)
     def _():
@@ -252,45 +256,65 @@
     prepare(kpw, vtw, kx, vx, 0, WINDOW, 0)
     near_pass((0,))
 
-    fifteen = kv.at[c, pl.ds(0, 15 * PIECE)]
-    remote(fifteen, fifteen, s3, r3, me).wait_recv()
-    half = remote(kv.at[c], kv.at[c], s4, r4, (z, x, y, 1 - c))
-    half.start()
-    half.wait_recv()
-    prepare(kps, vts, kv.at[0], kv.at[1], 0, 512, 0)
-
-    def far_scores(g, b, slot, special):
-        both = jnp.concatenate([kps[g, e] for e in range(2)], axis=0)
+    @pl.when(z > 0)
+    def _():
+        remote(piece[1], piece[1], s2.at[1], r2.at[1], me).wait_recv()
+        spread_plane(1)
+
+    fifteen = [kv.at[c, pl.ds(0, 15 * PIECE), cols[h]] for h in range(2)]
+    to_sibling = [
+        remote(kv.at[c, :, cols[h]], kv.at[c, :, cols[h]], s4.at[h], r4.at[h], (z, x, y, 1 - c)) for h in range(2)
+    ]
+
+    def gathered(h):
+        remote(fifteen[h], fifteen[h], s3.at[h], r3.at[h], me).wait_recv()
+        to_sibling[h].start()
+
+    def arrived(h):
+        to_sibling[h].wait_recv()
+        prepare(kps, vts, kv.at[0], kv.at[1], 0, 512, 0, (2 * h, 2 * h + 1))
+
+    gathered(0)
+    arrived(0)
+
+    def seen(b, kind):
+        if kind == 0:
+            return b, b > 0
+        return 4, kind == 1 and b == 0
+
+    def far_scores(g, b, slot, kind):
+        tiles, diagonal = seen(b, kind)
+        if tiles == 0:
+            return
+        n = tiles * 128
+        both = jnp.concatenate([kps[g, e, :n] for e in range(2)], axis=0)
         s = lax.dot_general(both, q_tile(g, b), NT, preferred_element_type=F32)
         for e in range(2):
-            part = s[e * 512 : e * 512 + 512]
-            if special:
-                index = lin * 4 + b
-                part = jnp.concatenate(
-                    [
-                        jnp.where(row - col <= 128 * (index - 1 - i), part[i * 128 : i * 128 + 128], NEG)
-                        for i in range(4)
-                    ],
-                    axis=0,
-                )
-            sb[slot, e] = part
+            part = s[e * n : e * n + n]
+            if diagonal:
+                last = jnp.where(own, part[n - 128 :], NEG)
+                part = last if tiles == 1 else jnp.concatenate([part[: n - 128], last], axis=0)
+            sb[slot, e, :n] = part
             tb[slot, e] = fold(part, jnp.maximum)
 
-    def far_weights(g, b, slot, late):
+    def far_weights(g, b, slot, kind, late):
+        tiles, _ = seen(b, kind)
+        n = tiles * 128
         for e in range(2):
             old = mw[g, b, e]
-            top = jnp.maximum(across(tb[slot, e], jnp.maximum), old)
+            top = jnp.maximum(across(tb[slot, e], jnp.maximum), old) if tiles else old
             scale = jnp.exp2(old - top)
             sink = jnp.exp2(sink_row(g, e) - top)
             dst = late_p.at[(g - EARLY) * 4 + b, e] if late else pb.at[slot, e]
-            acc = None
-            for r in range(0, 512, 64):
+            acc = jnp.zeros((8, 512), F32)
+            for r in range(0, n, 64):
                 w = jnp.exp2(sb[slot, e, r : r + 64] - tall(top, 8))
                 dst[r : r + 64, :] = w.astype(BF16)
                 if late:
-                    part = fold(w, jnp.add)
-                    acc = part if acc is None else acc + part
+                    acc = acc + fold(w, jnp.add)
             if late:
+                if n < 512:
+                    dst[n:512, :] = jnp.zeros((512 - n, 512), BF16)
                 inverse = 1.0 / (lw[g, b, e] * scale + across(acc, jnp.add))
                 sh[g, e] += sink * inverse
                 late_r[(g - EARLY) * 4 + b, e, 0] = scale * inverse
@@ -302,13 +326,17 @@
     def put(g, b, outs):
         both = jnp.concatenate(outs, axis=0)
         for p in range(4):
-            cols = pl.ds(pl.multiple_of(g * 512 + p * 128, 128), 128)
-            o_ref[b * 128 : b * 128 + 128, cols] = both[:, p * 128 : p * 128 + 128].T
-
-    def far_values(g, b, slot, share_at):
+            lanes = pl.ds(pl.multiple_of(g * 512 + p * 128, 128), 128)
+            ob[b * 128 : b * 128 + 128, lanes] = both[:, p * 128 : p * 128 + 128].T
+
+    def far_values(g, b, slot, share_at, kind):
         outs = []
-        for e in range(2):
-            o = jnp.dot(vts[g], pb[slot, e], preferred_element_type=F32)
+        n = seen(b, kind)[0] * 128
+        for e in range(2):
+            if n:
+                o = jnp.dot(vts[g, :, :n], pb[slot, e, :n], preferred_element_type=F32)
+            else:
+                o = jnp.zeros((80, 512), F32)
             scale = rb[slot, e, 0]
             inverse = 1.0 / (lw[g, b, e] * scale + o[64:72])
             sh[share_at, e] += rb[slot, e, 1] * inverse
@@ -324,43 +352,60 @@
         put(g, b, outs)
 
     sh[...] = jnp.zeros_like(sh)
-
-    def far_pass(special):
-        far_scores(0, 0, 0, special)
+    spans = (pl.ds(0, 2048), pl.ds(2048, 1024), pl.ds(3072, 1024))
+    stores = [pltpu.make_async_copy(ob.at[:, spans[i]], o_hbm.at[:, spans[i]], so.at[i]) for i in range(3)]
+
+    def store(i):
+        stores[i].start()
+
+
+    def far_pass(kind):
+        far_scores(0, 0, 0, kind)
 
         @pl.loop(0, EARLY)
         def _(g):
+            @pl.when(g == 1)
+            def _():
+                gathered(1)
+
             for b in range(4):
                 slot = b % 2
                 if b < 3:
-                    far_scores(g, b + 1, 1 - slot, special)
+                    far_scores(g, b + 1, 1 - slot, kind)
                 else:
-                    far_scores(g + 1, 0, 1 - slot, special)
+                    far_scores(jnp.minimum(g + 1, EARLY - 1), 0, 1 - slot, kind)
                 if b > 0:
-                    far_values(g, b - 1, 1 - slot, g)
+                    far_values(g, b - 1, 1 - slot, g, kind)
                 else:
-                    far_values(jnp.maximum(g - 1, 0), 3, 1 - slot, jnp.where(g > 0, g - 1, 8))
-                far_weights(g, b, slot, False)
-
-        far_values(EARLY - 1, 3, 1, EARLY - 1)
+                    far_values(jnp.maximum(g - 1, 0), 3, 1 - slot, jnp.where(g > 0, g - 1, 8), kind)
+                far_weights(g, b, slot, kind, False)
+
+        far_values(EARLY - 1, 3, 1, EARLY - 1, kind)
+        store(0)
+        arrived(1)
+        far_scores(EARLY, 0, 0, kind)
 
         @pl.loop(EARLY, 8)
         def _(g):
             for b in range(4):
                 slot = b % 2
                 if b < 3:
-                    far_scores(g, b + 1, 1 - slot, special)
+                    far_scores(g, b + 1, 1 - slot, kind)
                 else:
-                    far_scores(jnp.minimum(g + 1, 7), 0, 1 - slot, special)
-                far_weights(g, b, slot, True)
-
-    @pl.when(lin < 2)
-    def _():
-        far_pass(True)
+                    far_scores(jnp.minimum(g + 1, 7), 0, 1 - slot, kind)
+                far_weights(g, b, slot, kind, True)
+
+    @pl.when(lin == 0)
+    def _():
+        far_pass(0)
+
+    @pl.when(lin == 1)
+    def _():
+        far_pass(1)
 
     @pl.when(lin >= 2)
     def _():
-        far_pass(False)
+        far_pass(2)
 
     lane = lax.broadcasted_iota(jnp.int32, (8, 128), 1)
     mine = jnp.zeros((8, 128), F32)
@@ -378,6 +423,7 @@
         for b in range(4):
             late_values(g, b)
 
+    store(1)
     many = one.at[pl.ds(0, 15)]
     remote(many, many, s5, r5, me).wait_recv()
     two[zc] = jnp.sum(one[...], axis=0)
@@ -389,29 +435,45 @@
         for b in range(4):
             late_values(g, b)
 
+    store(2)
     lots = two.at[pl.ds(0, 15)]
     remote(lots, lots, s6, r6, me).wait_recv()
     total_ref[...] = jnp.sum(two[...], axis=0) * (1.0 / 131072)
 
     remote(many, many, s5, r5, me).wait_send()
     remote(lots, lots, s6, r6, me).wait_send()
-    half.wait_send()
-    remote(fifteen, fifteen, s3, r3, me).wait_send()
-
-    @pl.when(relay)
-    def _():
-        seven = kv.at[c, pl.ds(0, 7 * PIECE)]
-        remote(seven, seven, s2, r2, me).wait_send()
-
-    @pl.when(first)
-    def _():
-        sent = kv.at[:, pl.ds(0, 496)]
-        remote(sent, sent, s1, r1, me).wait_send()
+    for h in range(2):
+        to_sibling[h].wait_send()
+        remote(fifteen[h], fifteen[h], s3.at[h], r3.at[h], me).wait_send()
+
+        @pl.when(relay)
+        def _():
+            seven = kv.at[c, pl.ds(0, 7 * PIECE), cols[h]]
+            remote(seven, seven, s2.at[h], r2.at[h], me).wait_send()
+
+        @pl.when(first)
+        def _():
+            sent = kv.at[:, pl.ds(0, 496), cols[h]]
+            remote(sent, sent, s1.at[h], r1.at[h], me).wait_send()
+
+    for copy in stores:
+        copy.wait()
 
     @pl.when(lin < 255)
     def _():
         for i, ref in enumerate((kx, vx)):
             remote(ref.at[pl.ds(512, WINDOW)], ref.at[pl.ds(0, WINDOW)], se.at[i], re.at[i], me).wait_send()
+
+
+def finish_kernel(a_ref, t_ref, o_ref, share_ref, sem):
+    copies = [
+        pltpu.make_async_copy(a_ref.at[pl.ds(i * 64, 64)], o_ref.at[pl.ds(i * 64, 64)], sem.at[i]) for i in range(8)
+    ]
+    for copy in copies:
+        copy.start()
+    share_ref[...] = t_ref[0, 0:64]
+    for copy in copies:
+        copy.wait()
 
 
 def local(queries, keys, values, sink_logits):
@@ -421,9 +483,10 @@
     attended, total = pl.pallas_call(
         kernel,
         in_specs=[pl.BlockSpec(memory_space=pltpu.SMEM), hbm, hbm, hbm],
-        out_specs=[vmem, vmem],
+        out_specs=[hbm, vmem],
         out_shape=[jax.ShapeDtypeStruct((512, 4096), BF16), jax.ShapeDtypeStruct((8, 128), F32)],
         scratch_shapes=[
+            pltpu.VMEM((512, 4096), BF16),
             pltpu.VMEM((512, 4096), BF16),
             pltpu.VMEM((640, 512), BF16),
             pltpu.VMEM((640, 512), BF16),
@@ -446,15 +509,22 @@
             pltpu.VMEM((16, 8, 128), F32),
             dma(()),
             dma((2,)),
+            dma((3,)),
         ]
-        + [dma(())] * 8
+        + [dma((2,))] * 8
         + [dma((2,))] * 2
         + [dma(())] * 4,
         compiler_params=pltpu.CompilerParams(
             collective_id=0, has_side_effects=True, vmem_limit_bytes=60 << 20
         ),
     )(sink_logits, queries, keys, values)
-    return attended, total[0, :64]
+    return pl.pallas_call(
+        finish_kernel,
+        in_specs=[hbm, vmem],
+        out_specs=[hbm, vmem],
+        out_shape=[jax.ShapeDtypeStruct((512, 4096), BF16), jax.ShapeDtypeStruct((64,), F32)],
+        scratch_shapes=[dma((8,))],
+    )(attended, total)
 
 
 def solution(mesh):

time: 74.3 us -> 193 us (2.60)
  Pallas kernels: 67.6 us -> 192 us
  local copies, waits for them, and re-layouts: 5.88 us -> 0 us
    pallas_call x0 -> x1, Pallas kernels: none -> 129 us  [local(): pl.pallas_call(finish_kernel, in_specs=[hbm, vmem], out_specs=[hbm, vmem]...]
    pallas_call x1, Pallas kernels: 67.6 us -> 62.7 us  [local(): pl.pallas_call(kernel, in_specs=[pl.BlockSpec(memory_space=pltpu.SMEM), h...]
    unnamed x1 -> x0, local copies, waits for them, and re-layouts: 4.7 us -> none
where the time goes in v3:
time: 193 us
  Pallas kernels  192 us (99%)
    pallas_call x1, Pallas kernels, local(): pl.pallas_call(finish_kernel, in_specs=[hbm, vmem], out_specs=[hbm, vmem]...  129 us
    pallas_call x1, Pallas kernels, local(): pl.pallas_call(kernel, in_specs=[pl.BlockSpec(memory_space=pltpu.SMEM), h...  62.7 us

profile of v3, /device:TPU:1, one launch (start us, length us, event | category | flops | bytes accessed | tf_op | source)
XLA Modules:
  0.0 192.9 jit_solution(6681351334120831966)
XLA Ops:
  0.6 62.7 %shard_map.59 = (bf16[512,4096]{1,0:T(8,128)(2,1)}, f32[8,128]{1,0:T(8,128)}) custom-call(f32[64]{0:T(128)} %sink_ref.1, bf16[512,4096]{1,0:T(8,128)(2,1)} %q_hbm.1, bf16[512,512]{1,0:T(8,128)(2,1)} %k_hbm.1, bf16[512,512]{1,0:T(8,128)(2,1)} %v_hbm.1), custom_call_target="tpu_custom_call" | custom-call | tf_op jit(solution)/shard_map/pallas_call | solution.py:483
  63.3 129.4 %shard_map.60 = (bf16[512,4096]{1,0:T(8,128)(2,1)}, f32[64]{0:T(128)}) custom-call(bf16[512,4096]{1,0:T(8,128)(2,1)} %get-tuple-element.4.a_ref, f32[8,128]{1,0:T(8,128)} %get-tuple-element.5.t_ref), custom_call_target="tpu_custom_call" | custom-call | tf_op jit(solution)/shard_map/pallas_call | solution.py:521

commit v4 on v3

--- a/solution.py
+++ b/solution.py
@@ -465,14 +465,17 @@
             remote(ref.at[pl.ds(512, WINDOW)], ref.at[pl.ds(0, WINDOW)], se.at[i], re.at[i], me).wait_send()
 
 
-def finish_kernel(a_ref, t_ref, o_ref, share_ref, sem):
-    copies = [
-        pltpu.make_async_copy(a_ref.at[pl.ds(i * 64, 64)], o_ref.at[pl.ds(i * 64, 64)], sem.at[i]) for i in range(8)
-    ]
-    for copy in copies:
+def finish_kernel(a_ref, t_ref, o_ref, share_ref, buf, come, go):
+    parts = [pl.ds(i * 64, 64) for i in range(8)]
+    loads = [pltpu.make_async_copy(a_ref.at[part], buf.at[part], come.at[i]) for i, part in enumerate(parts)]
+    stores = [pltpu.make_async_copy(buf.at[part], o_ref.at[part], go.at[i]) for i, part in enumerate(parts)]
+    for copy in loads:
         copy.start()
     share_ref[...] = t_ref[0, 0:64]
-    for copy in copies:
+    for load, store in zip(loads, stores):
+        load.wait()
+        store.start()
+    for copy in stores:
         copy.wait()
 
 
@@ -523,7 +526,7 @@
         in_specs=[hbm, vmem],
         out_specs=[hbm, vmem],
         out_shape=[jax.ShapeDtypeStruct((512, 4096), BF16), jax.ShapeDtypeStruct((64,), F32)],
-        scratch_shapes=[dma((8,))],
+        scratch_shapes=[pltpu.VMEM((512, 4096), BF16), dma((8,)), dma((8,))],
     )(attended, total)
 
 

time: 193 us -> 68.4 us (0.35)
  Pallas kernels: 192 us -> 67.4 us
    pallas_call x1, Pallas kernels: 129 us -> 4.76 us  [local(): pl.pallas_call(finish_kernel, in_specs=[hbm, vmem], out_specs=[hbm, vmem]...]
where the time goes in v4:
time: 68.4 us; the launch traced here: 68.2 us
  Pallas kernels  67.4 us (99%)
  between operations  0.8 us (1%)
    pallas_call x1, Pallas kernels, local(): pl.pallas_call(kernel, in_specs=[pl.BlockSpec(memory_space=pltpu.SMEM), h...  62.7 us
    pallas_call x1, Pallas kernels, local(): pl.pallas_call(finish_kernel, in_specs=[hbm, vmem], out_specs=[hbm, vmem]...  4.76 us

profile of v4, /device:TPU:1, one launch (start us, length us, event | category | flops | bytes accessed | tf_op | source)
XLA Modules:
  0.0 68.2 jit_solution(4941494384371131947)
XLA Ops:
  0.6 62.7 %shard_map.59 = (bf16[512,4096]{1,0:T(8,128)(2,1)}, f32[8,128]{1,0:T(8,128)}) custom-call(f32[64]{0:T(128)} %sink_ref.1, bf16[512,4096]{1,0:T(8,128)(2,1)} %q_hbm.1, bf16[512,512]{1,0:T(8,128)(2,1)} %k_hbm.1, bf16[512,512]{1,0:T(8,128)(2,1)} %v_hbm.1), custom_call_target="tpu_custom_call" | custom-call | tf_op jit(solution)/shard_map/pallas_call | solution.py:486
  63.3 4.8 %shard_map.60 = (bf16[512,4096]{1,0:T(8,128)(2,1)}, f32[64]{0:T(128)}) custom-call(bf16[512,4096]{1,0:T(8,128)(2,1)} %get-tuple-element.4.a_ref, f32[8,128]{1,0:T(8,128)} %get-tuple-element.5.t_ref), custom_call_target="tpu_custom_call" | custom-call | tf_op jit(solution)/shard_map/pallas_call | solution.py:524

commit v5 on v4

--- a/solution.py
+++ b/solution.py
@@ -70,7 +70,7 @@
 def kernel(
     sink_ref, q_hbm, k_hbm, v_hbm, o_hbm, total_ref,
     qb, ob, kx, vx, kv, kpw, kps, vtw, vts, ow, mw, lw, sb, tb, pb, rb, late_p, late_r, sh, one, two,
-    sq, sk, so, s1, r1, s2, r2, s3, r3, s4, r4, se, re, s5, r5, s6, r6,
+    ready, sq, sk, so, s1, r1, s2, r2, s3, r3, s4, r4, se, re, s5, r5, s6, r6,
 ):
     z, x, y, c = (lax.axis_index(a) for a in AXES)
     lin = ((z * 4 + x) * 4 + y) * 2 + c
@@ -105,19 +105,30 @@
 
     barrier = pltpu.get_barrier_semaphore()
 
-    @pl.when(relay & (lin > 0))
+    @pl.when(relay & (c == 1))
     def _():
         signal(barrier, (0, 0, 0, 0))
-
-    @pl.when(lin > 0)
-    def _():
-        signal(barrier, coords(lin - 1))
 
     for step in range(1, 16):
         signal(barrier, plane(step))
-        signal(barrier, column(step))
-
-    pl.semaphore_wait(barrier, 30 + jnp.where(lin < 255, 1, 0) + jnp.where(first, 31, 0))
+    signal(barrier, (z, x, y, 1 - c))
+
+    @pl.when((c == 0) & (lin > 0))
+    def _():
+        signal(barrier, coords(lin - 1))
+
+    @pl.when(relay)
+    def _():
+        for zz in range(1, 8):
+            signal(barrier, (zz, x, y, c))
+
+    from_next = jnp.where((c == 1) & (lin < 255), 1, 0)
+    pl.semaphore_wait(barrier, 16 + from_next + jnp.where(first, 16, 0) + jnp.where(relay, 0, 1))
+
+    @pl.when(z > 0)
+    def _():
+        signal(ready, (0, x, y, c))
+
     for copy in loads:
         copy.wait()
 
@@ -235,6 +246,7 @@
 
     @pl.when(relay)
     def _():
+        pl.semaphore_wait(ready, 7)
         for h in range(2):
             remote(piece[h], piece[h], s2.at[h], r1.at[h], me).wait_recv()
             for zz in range(1, 8):
@@ -510,6 +522,7 @@
             pltpu.VMEM((9, 2, 8, 512), F32),
             pltpu.VMEM((16, 8, 128), F32),
             pltpu.VMEM((16, 8, 128), F32),
+            pltpu.SemaphoreType.REGULAR,
             dma(()),
             dma((2,)),
             dma((3,)),

time: 68.4 us -> 67.3 us (0.984)
  Pallas kernels: 67.4 us -> 66.3 us
    pallas_call x1, Pallas kernels: 62.7 us -> 61.6 us  [local(): pl.pallas_call(kernel, in_specs=[pl.BlockSpec(memory_space=pltpu.SMEM), h...]
where the time goes in v5:
time: 67.3 us; the launch traced here: 67.1 us
  Pallas kernels  66.3 us (99%)
  between operations  0.8 us (1%)
    pallas_call x1, Pallas kernels, local(): pl.pallas_call(kernel, in_specs=[pl.BlockSpec(memory_space=pltpu.SMEM), h...  61.6 us
    pallas_call x1, Pallas kernels, local(): pl.pallas_call(finish_kernel, in_specs=[hbm, vmem], out_specs=[hbm, vmem]...  4.76 us

profile of v5, /device:TPU:1, one launch (start us, length us, event | category | flops | bytes accessed | tf_op | source)
XLA Modules:
  0.0 67.1 jit_solution(4469872012554535796)
XLA Ops:
  0.6 61.6 %shard_map.59 = (bf16[512,4096]{1,0:T(8,128)(2,1)}, f32[8,128]{1,0:T(8,128)}) custom-call(f32[64]{0:T(128)} %sink_ref.1, bf16[512,4096]{1,0:T(8,128)(2,1)} %q_hbm.1, bf16[512,512]{1,0:T(8,128)(2,1)} %k_hbm.1, bf16[512,512]{1,0:T(8,128)(2,1)} %v_hbm.1), custom_call_target="tpu_custom_call" | custom-call | tf_op jit(solution)/shard_map/pallas_call | solution.py:498
  62.2 4.8 %shard_map.60 = (bf16[512,4096]{1,0:T(8,128)(2,1)}, f32[64]{0:T(128)}) custom-call(bf16[512,4096]{1,0:T(8,128)(2,1)} %get-tuple-element.4.a_ref, f32[8,128]{1,0:T(8,128)} %get-tuple-element.5.t_ref), custom_call_target="tpu_custom_call" | custom-call | tf_op jit(solution)/shard_map/pallas_call | solution.py:537

commit v6 on v5

--- a/solution.py
+++ b/solution.py
@@ -70,7 +70,7 @@
 def kernel(
     sink_ref, q_hbm, k_hbm, v_hbm, o_hbm, total_ref,
     qb, ob, kx, vx, kv, kpw, kps, vtw, vts, ow, mw, lw, sb, tb, pb, rb, late_p, late_r, sh, one, two,
-    ready, sq, sk, so, s1, r1, s2, r2, s3, r3, s4, r4, se, re, s5, r5, s6, r6,
+    extra, sq, sk, so, r0, s1, r1, s2, r2, s3, r3, s4, r4, se, re, s5, r5, s6, r6,
 ):
     z, x, y, c = (lax.axis_index(a) for a in AXES)
     lin = ((z * 4 + x) * 4 + y) * 2 + c
@@ -117,17 +117,20 @@
     def _():
         signal(barrier, coords(lin - 1))
 
-    @pl.when(relay)
-    def _():
-        for zz in range(1, 8):
-            signal(barrier, (zz, x, y, c))
-
+    corner = (x == 0) & (y == 0)
+
+    @pl.when((z > 0) & corner)
+    def _():
+        signal(barrier, (0, 0, 0, 1))
+
+    @pl.when((z > 0) & jnp.logical_not(corner))
+    def _():
+        signal(barrier, (0, x, y, c))
+
+    helper = lin == 1
     from_next = jnp.where((c == 1) & (lin < 255), 1, 0)
-    pl.semaphore_wait(barrier, 16 + from_next + jnp.where(first, 16, 0) + jnp.where(relay, 0, 1))
-
-    @pl.when(z > 0)
-    def _():
-        signal(ready, (0, x, y, c))
+    from_column = jnp.where(relay & (lin > 1), 7, 0) + jnp.where(helper, 14, 0)
+    pl.semaphore_wait(barrier, 16 + from_next + jnp.where(first, 16, 0) + from_column)
 
     for copy in loads:
         copy.wait()
@@ -141,6 +144,7 @@
                     dst = kv.at[cc, pl.ds(p * PIECE, PIECE), cols[h]]
                     if cc == 0 and p == 0:
                         pltpu.make_async_copy(src, dst, r1.at[h]).start()
+                        remote(src, extra.at[:, cols[h]], s1.at[h], r0.at[h], (0, 0, 0, 1)).start()
                     else:
                         remote(src, dst, s1.at[h], r1.at[h], (0, p // 4, p % 4, cc)).start()
         for i, ref in enumerate((kx, vx)):
@@ -242,23 +246,36 @@
     q_load.wait()
     pb[...] = jnp.zeros_like(pb)
     rb[...] = jnp.zeros_like(rb)
-    near_pass((3, 2))
 
     @pl.when(relay)
     def _():
-        pl.semaphore_wait(ready, 7)
         for h in range(2):
             remote(piece[h], piece[h], s2.at[h], r1.at[h], me).wait_recv()
-            for zz in range(1, 8):
-                remote(piece[h], piece[h], s2.at[h], r2.at[h], (zz, x, y, c)).start()
+
+            @pl.when(lin > 0)
+            def _():
+                for zz in range(1, 8):
+                    remote(piece[h], piece[h], s2.at[h], r2.at[h], (zz, x, y, c)).start()
+
+            @pl.when(helper)
+            def _():
+                spare = extra.at[:, cols[h]]
+                remote(spare, spare, s2.at[h], r0.at[h], me).wait_recv()
+                for zz in range(1, 8):
+                    target = kv.at[0, pl.ds(0, PIECE), cols[h]]
+                    remote(spare, target, s2.at[h], r2.at[h], (zz, 0, 0, 0)).start()
+
             spread_plane(h)
 
-    near_pass((1,))
+    near_pass((3,))
 
     @pl.when(z > 0)
     def _():
-        remote(piece[0], piece[0], s2.at[0], r2.at[0], me).wait_recv()
-        spread_plane(0)
+        for h in range(2):
+            remote(piece[h], piece[h], s2.at[h], r2.at[h], me).wait_recv()
+            spread_plane(h)
+
+    near_pass((2, 1))
 
     @pl.when(lin > 0)
     def _():
@@ -266,12 +283,6 @@
             remote(ref.at[pl.ds(512, WINDOW)], ref.at[pl.ds(0, WINDOW)], se.at[i], re.at[i], me).wait_recv()
 
     prepare(kpw, vtw, kx, vx, 0, WINDOW, 0)
-    near_pass((0,))
-
-    @pl.when(z > 0)
-    def _():
-        remote(piece[1], piece[1], s2.at[1], r2.at[1], me).wait_recv()
-        spread_plane(1)
 
     fifteen = [kv.at[c, pl.ds(0, 15 * PIECE), cols[h]] for h in range(2)]
     to_sibling = [
@@ -287,6 +298,7 @@
         prepare(kps, vts, kv.at[0], kv.at[1], 0, 512, 0, (2 * h, 2 * h + 1))
 
     gathered(0)
+    near_pass((0,))
     arrived(0)
 
     def seen(b, kind):
@@ -458,14 +470,19 @@
         to_sibling[h].wait_send()
         remote(fifteen[h], fifteen[h], s3.at[h], r3.at[h], me).wait_send()
 
-        @pl.when(relay)
+        @pl.when(helper)
+        def _():
+            twice = kv.at[c, pl.ds(0, 14 * PIECE), cols[h]]
+            remote(twice, twice, s2.at[h], r2.at[h], me).wait_send()
+
+        @pl.when(relay & (lin > 1))
         def _():
             seven = kv.at[c, pl.ds(0, 7 * PIECE), cols[h]]
             remote(seven, seven, s2.at[h], r2.at[h], me).wait_send()
 
         @pl.when(first)
         def _():
-            sent = kv.at[:, pl.ds(0, 496), cols[h]]
+            sent = kv.at[:, :, cols[h]]
             remote(sent, sent, s1.at[h], r1.at[h], me).wait_send()
 
     for copy in stores:
@@ -522,10 +539,11 @@
             pltpu.VMEM((9, 2, 8, 512), F32),
             pltpu.VMEM((16, 8, 128), F32),
             pltpu.VMEM((16, 8, 128), F32),
-            pltpu.SemaphoreType.REGULAR,
+            pltpu.VMEM((PIECE, 512), BF16),
             dma(()),
             dma((2,)),
             dma((3,)),
+            dma((2,)),
         ]
         + [dma((2,))] * 8
         + [dma((2,))] * 2

time: 67.3 us -> 74 us (1.100)
  Pallas kernels: 66.3 us -> 73 us
    pallas_call x1, Pallas kernels: 61.6 us -> 68.3 us  [local(): pl.pallas_call(kernel, in_specs=[pl.BlockSpec(memory_space=pltpu.SMEM), h...]
where the time goes in v6:
time: 74 us; the launch traced here: 73.8 us
  Pallas kernels  73 us (99%)
  between operations  0.8 us (1%)
    pallas_call x1, Pallas kernels, local(): pl.pallas_call(kernel, in_specs=[pl.BlockSpec(memory_space=pltpu.SMEM), h...  68.3 us
    pallas_call x1, Pallas kernels, local(): pl.pallas_call(finish_kernel, in_specs=[hbm, vmem], out_specs=[hbm, vmem]...  4.76 us

profile of v6, /device:TPU:1, one launch (start us, length us, event | category | flops | bytes accessed | tf_op | source)
XLA Modules:
  0.0 73.8 jit_solution(986699407859445920)
XLA Ops:
  0.6 68.3 %shard_map.59 = (bf16[512,4096]{1,0:T(8,128)(2,1)}, f32[8,128]{1,0:T(8,128)}) custom-call(f32[64]{0:T(128)} %sink_ref.1, bf16[512,4096]{1,0:T(8,128)(2,1)} %q_hbm.1, bf16[512,512]{1,0:T(8,128)(2,1)} %k_hbm.1, bf16[512,512]{1,0:T(8,128)(2,1)} %v_hbm.1), custom_call_target="tpu_custom_call" | custom-call | tf_op jit(solution)/shard_map/pallas_call | solution.py:515
  68.9 4.8 %shard_map.60 = (bf16[512,4096]{1,0:T(8,128)(2,1)}, f32[64]{0:T(128)}) custom-call(bf16[512,4096]{1,0:T(8,128)(2,1)} %get-tuple-element.4.a_ref, f32[8,128]{1,0:T(8,128)} %get-tuple-element.5.t_ref), custom_call_target="tpu_custom_call" | custom-call | tf_op jit(solution)/shard_map/pallas_call | solution.py:555

commit v7 on v5

--- a/solution.py
+++ b/solution.py
@@ -251,7 +251,8 @@
             remote(piece[h], piece[h], s2.at[h], r1.at[h], me).wait_recv()
             for zz in range(1, 8):
                 remote(piece[h], piece[h], s2.at[h], r2.at[h], (zz, x, y, c)).start()
-            spread_plane(h)
+            if h == 0:
+                spread_plane(0)
 
     near_pass((1,))
 
@@ -267,11 +268,6 @@
 
     prepare(kpw, vtw, kx, vx, 0, WINDOW, 0)
     near_pass((0,))
-
-    @pl.when(z > 0)
-    def _():
-        remote(piece[1], piece[1], s2.at[1], r2.at[1], me).wait_recv()
-        spread_plane(1)
 
     fifteen = [kv.at[c, pl.ds(0, 15 * PIECE), cols[h]] for h in range(2)]
     to_sibling = [
@@ -287,6 +283,12 @@
         prepare(kps, vts, kv.at[0], kv.at[1], 0, 512, 0, (2 * h, 2 * h + 1))
 
     gathered(0)
+
+    @pl.when(z > 0)
+    def _():
+        remote(piece[1], piece[1], s2.at[1], r2.at[1], me).wait_recv()
+
+    spread_plane(1)
     arrived(0)
 
     def seen(b, kind):

time: 67.3 us -> 68.2 us (1.013)
  Pallas kernels: 66.3 us -> 67.2 us
    pallas_call x1, Pallas kernels: 61.6 us -> 62.5 us  [local(): pl.pallas_call(kernel, in_specs=[pl.BlockSpec(memory_space=pltpu.SMEM), h...]
where the time goes in v7:
time: 68.2 us; the launch traced here: 68 us
  Pallas kernels  67.2 us (99%)
  between operations  0.8 us (1%)
    pallas_call x1, Pallas kernels, local(): pl.pallas_call(kernel, in_specs=[pl.BlockSpec(memory_space=pltpu.SMEM), h...  62.5 us
    pallas_call x1, Pallas kernels, local(): pl.pallas_call(finish_kernel, in_specs=[hbm, vmem], out_specs=[hbm, vmem]...  4.76 us

profile of v7, /device:TPU:1, one launch (start us, length us, event | category | flops | bytes accessed | tf_op | source)
XLA Modules:
  0.0 68.0 jit_solution(18161515149241000992)
XLA Ops:
  0.6 62.5 %shard_map.59 = (bf16[512,4096]{1,0:T(8,128)(2,1)}, f32[8,128]{1,0:T(8,128)}) custom-call(f32[64]{0:T(128)} %sink_ref.1, bf16[512,4096]{1,0:T(8,128)(2,1)} %q_hbm.1, bf16[512,512]{1,0:T(8,128)(2,1)} %k_hbm.1, bf16[512,512]{1,0:T(8,128)(2,1)} %v_hbm.1), custom_call_target="tpu_custom_call" | custom-call | tf_op jit(solution)/shard_map/pallas_call | solution.py:500
  63.1 4.8 %shard_map.60 = (bf16[512,4096]{1,0:T(8,128)(2,1)}, f32[64]{0:T(128)}) custom-call(bf16[512,4096]{1,0:T(8,128)(2,1)} %get-tuple-element.4.a_ref, f32[8,128]{1,0:T(8,128)} %get-tuple-element.5.t_ref), custom_call_target="tpu_custom_call" | custom-call | tf_op jit(solution)/shard_map/pallas_call | solution.py:539
